TPU v7x, 128 devices: a whole 4x4x4 slice. The times are simulated.
128 devices in a mesh: pa: 16 (over x_lo, y, core), row: 8 (over z, x_hi).
Axes of the slice: x: 4 (x_hi: 2, x_lo: 2; x = x_hi * 2 + x_lo), y: 4, z: 4, core: 2. Of those that a mesh axis runs over, the one named last changes fastest.
Arguments:
- echoes: bfloat16 [2, 4096, 256, 128], P(None, 'row', 'pa'), may hold values from -6 to 6
- chirp_phase: float32 [256], replicated, may hold values from -3.140625 to 3.140625
Outputs:
- covariance: float32 [256, 2, 128, 128], P(('pa', 'row'))
All inputs are finite; a program needn't handle non-finite values.
Results may differ from a plain program's by a relative error of at most 0.0016.
Values may be sent and summed in bfloat16 or wider, within the bound.
No kernel may reach another device: no remote copies, remote signals or barrier semaphores. Data moves between devices by JAX's collectives and lax.ppermute only.
A program may use at most 64 MiB of HBM per device.

v0:
```python
import math

import jax
import jax.numpy as jnp
from jax import lax
from jax.sharding import PartitionSpec as P


def shifted(array, axis, by):
    devices = lax.axis_size(axis)
    pairs = [(i, i + by) for i in range(devices) if 0 <= i + by < devices]
    return lax.ppermute(array, axis, pairs)


def filter_parts(chirp_phase):
    scaling = 1.0 / math.sqrt(chirp_phase.shape[0])
    real_part = (jnp.cos(chirp_phase) * scaling).astype(jnp.bfloat16)
    imag_part = (-jnp.sin(chirp_phase) * scaling).astype(jnp.bfloat16)
    return (real_part, imag_part)


def banded_filter(real_part, imag_part, out_rows):
    tap_count = real_part.shape[0]
    in_rows = out_rows + tap_count - 1

    def banded(values):
        padded = jnp.concatenate([values, jnp.zeros((in_rows + 1 - tap_count,), values.dtype)])
        repeated = jnp.tile(padded, out_rows)[: out_rows * in_rows]
        return repeated.reshape(out_rows, in_rows)

    real_band = banded(real_part)
    imag_band = banded(imag_part)
    upper_half = jnp.concatenate([real_band, -imag_band], axis=1)
    lower_half = jnp.concatenate([imag_band, real_band], axis=1)
    return jnp.concatenate([upper_half, lower_half], axis=0)


def doppler_matrix(pulses):
    indices = jnp.arange(pulses, dtype=jnp.int32)
    products = indices[:, None] * indices[None, :] % pulses
    angles = 2.0 * math.pi / pulses * products.astype(jnp.float32)
    scaling = 1.0 / math.sqrt(pulses)
    real_part = (jnp.cos(angles) * scaling).astype(jnp.bfloat16)
    imag_part = (-jnp.sin(angles) * scaling).astype(jnp.bfloat16)
    upper_half = jnp.stack([real_part, -imag_part], axis=1)
    lower_half = jnp.stack([imag_part, real_part], axis=1)
    return jnp.stack([upper_half, lower_half], axis=0)


def hermitian_parts(blocks_product):
    real_sum = blocks_product[:, 0, :, 0, :] + blocks_product[:, 1, :, 1, :]
    imag_sum = blocks_product[:, 1, :, 0, :] - blocks_product[:, 0, :, 1, :]
    return jnp.stack([real_sum, imag_sum], axis=1)


def per_device(echoes, chirp_phase):
    gates_dev = echoes.shape[1]
    pulses_dev = echoes.shape[2]
    element_count = echoes.shape[3]
    tap_count = chirp_phase.shape[0]
    pa_count = lax.axis_size("pa")
    row_count = lax.axis_size("row")
    pulses = pulses_dev * pa_count
    total_gates = gates_dev * row_count
    real_part, imag_part = filter_parts(chirp_phase)
    following = shifted(echoes[:, : tap_count - 1], "row", -1)
    extended = jnp.concatenate([echoes, following], axis=1)
    banded = banded_filter(real_part, imag_part, gates_dev)
    flattened = extended.reshape(2 * (gates_dev + tap_count - 1), pulses_dev * element_count)
    compressed = jnp.dot(banded, flattened, preferred_element_type=jnp.float32).astype(jnp.bfloat16)
    compressed = compressed.reshape(2, gates_dev, pulses_dev, element_count)
    turned = lax.all_to_all(compressed, "pa", split_axis=1, concat_axis=2, tiled=True)
    matrix = doppler_matrix(pulses)
    spectrum = jnp.einsum(
        "xbyp,ygpe->xgbe", matrix, turned, preferred_element_type=jnp.float32
    ).astype(jnp.bfloat16)
    owned_bins = lax.all_to_all(spectrum, ("pa", "row"), split_axis=2, concat_axis=1, tiled=True)
    blocks_product = jnp.einsum(
        "xgbi,ygbj->bxiyj", owned_bins, owned_bins, preferred_element_type=jnp.float32
    )
    covariance = hermitian_parts(blocks_product) / total_gates
    return covariance


def solution(mesh):
    placed = (P(None, "row", "pa", None), P())
    return jax.shard_map(
        per_device,
        mesh=mesh,
        in_specs=placed,
        out_specs=P(("pa", "row"), None, None, None),
        check_vma=False,
    )
```

profile of v0, /device:TPU:0, one launch (start us, length us, event | category | flops | bytes accessed | tf_op | source)
XLA Modules:
  0.0 238.0 jit_solution(549988020899475333)
XLA Ops:
  0.0 3.3 %slice.23 = bf16[2,255,16,128]{3,2,1,0:T(8,128)(2,1)} slice(bf16[2,512,16,128]{3,2,1,0:T(8,128)(2,1)} %param.2), slice={[0:2], [0:255], [0:16], [0:128]} | slice | bytes 4177920 | tf_op jit(solution)/shard_map/slice | solution.py:66
  3.3 1.3 collective-permute-start
  4.6 0.7 multiply_convert_fusion.2
  5.3 0.1 tile.8
  5.4 0.7 tile.9
  6.0 1.7 reshape.140
  7.8 0.1 tile.20
  7.8 0.7 tile.21
  8.5 1.7 reshape.141
  10.2 0.1 neg.33
  10.4 43.7 %collective-permute-done = bf16[2,255,16,128]{3,2,1,0:T(8,128)(2,1)} collective-permute-done((bf16[2,255,16,128]{3,2,1,0:T(8,128)(2,1)}, bf16[2,255,16,128]{3,2,1,0:T(8,128)(2,1)}, u32[]{:S(2)}, u32[]{:S(2)}) %collective-permute-start) | collective-permute-done | bytes 2088992 | tf_op jit(solution)/shard_map/ppermute | solution.py:12
  54.1 3.4 %pad_maximum_fusion = bf16[2,767,16,128]{3,2,1,0:T(8,128)(2,1)S(1)} fusion(bf16[2,255,16,128]{3,2,1,0:T(8,128)(2,1)} %collective-permute-done, bf16[2,512,16,128]{3,2,1,0:T(8,128)(2,1)} %param.2), kind=kLoop, calls=%fused_computation.1 | loop fusion | flops 3141632 | bytes 12566528 | tf_op jit(solution)/shard_map/concatenate | solution.py:67
  57.4 1.3 pad.22
  58.8 3.2 %copy.46 = bf16[192,8,16,128]{3,1,2,0:T(8,128)(2,1)S(1)} copy(bf16[192,8,16,128]{3,2,1,0:T(8,128)(2,1)S(1)} %bitcast.60) | data formatting | bytes 12582912
  62.0 17.8 %convert_bitcast_fusion = bf16[128,8,16,128]{3,1,2,0:T(8,128)(2,1)S(1)} fusion(bf16[1534,2048]{1,0:T(8,128)(2,1)S(1)} %bitcast.64, bf16[512,767]{1,0:T(8,128)(2,1)S(1)} %reshape.140, bf16[512,767]{1,0:T(8,128)(2,1)S(1)} %reshape.141, bf16[512,767]{1,0:T(8,128)(2,1)S(1)} %neg.33), kind=kOutput, calls=%fused_computation.5 | convolution fusion | flops 6448726016 | bytes 12833792 | tf_op jit(solution)/shard_map/dot_general | solution.py:70
  79.8 1.4 copy.47
  81.2 2.7 %copy.24 = bf16[2,512,16,128]{3,2,0,1:T(8,128)(2,1)} copy(bf16[2,512,16,128]{3,2,1,0:T(8,128)(2,1)S(1)} %bitcast.62) | data formatting | bytes 8388608 | tf_op jit(solution)/shard_map/reshape | solution.py:71
  83.9 5.8 %all-to-all-start = ((bf16[2,512,16,128]{3,2,0,1:T(8,128)(2,1)}), bf16[2,512,16,128]{3,2,0,1:T(8,128)(2,1)}, u32[]{:S(2)}, u32[]{:S(2)}) async-start(bf16[2,512,16,128]{3,2,0,1:T(8,128)(2,1)} %copy.24), calls=%async_computation | async-start | bytes 8388608 | tf_op jit(solution)/shard_map/all_to_all | solution.py:72
  89.7 1.0 fusion.20
  90.7 1.1 multiply_convert_fusion
  91.9 54.6 %all-to-all-done = bf16[2,512,16,128]{3,2,0,1:T(8,128)(2,1)} async-done(((bf16[2,512,16,128]{3,2,0,1:T(8,128)(2,1)}), bf16[2,512,16,128]{3,2,0,1:T(8,128)(2,1)}, u32[]{:S(2)}, u32[]{:S(2)}) %all-to-all-start) | async-done | bytes 4194336 | tf_op jit(solution)/shard_map/all_to_all | solution.py:72
  146.5 3.4 %copy.26 = bf16[2,32,16,16,128]{4,3,2,1,0:T(8,128)(2,1)S(1)} copy(bf16[2,32,16,16,128]{4,3,0,1,2:T(8,128)(2,1)} %bitcast.2) | data formatting | bytes 8388608 | tf_op jit(solution)/shard_map/all_to_all | solution.py:72
  149.9 4.4 %fusion = bf16[2,32,256,128]{2,3,0,1:T(8,128)(2,1)} fusion(bf16[2,32,256,128,1]{3,2,1,0,4:T(8,128)(2,1)S(1)} %bitcast.65, bf16[1,256,2,256]{3,1,2,0:T(8,128)(2,1)S(1)} %get-tuple-element.6, bf16[1,256,2,256]{3,1,2,0:T(8,128)(2,1)S(1)} %get-tuple-element.5), kind=kOutput, calls=%fused_computation.2 | convolution fusion | flops 2150629376 | bytes 8912896 | tf_op jit(solution)/shard_map/xbyp,ygpe->xgbe/dot_general | solution.py:74
  154.3 11.2 %copy.28 = bf16[2,32,256,128]{3,0,1,2:T(2,128)(2,1)} copy(bf16[2,32,256,128]{2,3,0,1:T(8,128)(2,1)} %fusion) | data formatting | bytes 8388608 | tf_op jit(solution)/shard_map/convert_element_type | solution.py:76
  165.5 68.4 %all_to_all.36 = bf16[2,32,256,128]{3,0,1,2:T(2,128)(2,1)S(1)} all-to-all(bf16[2,32,256,128]{3,0,1,2:T(2,128)(2,1)} %copy.28), channel_id=1, replica_groups=mesh['pa'=16,'row'=8] {'pa','row'}, dimensions={2} | all-to-all | bytes 8388608 | tf_op jit(solution)/shard_map/all_to_all | solution.py:77
  233.9 0.6 copy.29
  234.6 0.8 copy.30
  235.4 1.8 fusion.23
  237.3 0.7 copy.34
  (6 shorter events, 0.1 us)
Async XLA Ops:
  3.3 50.8 %collective-permute-start = (bf16[2,255,16,128]{3,2,1,0:T(8,128)(2,1)}, bf16[2,255,16,128]{3,2,1,0:T(8,128)(2,1)}, u32[]{:S(2)}, u32[]{:S(2)}) collective-permute-start(bf16[2,255,16,128]{3,2,1,0:T(8,128)(2,1)} %slice.23), channel_id=1, source_target_pairs={{1,0},{2,1},{3,2},{4,3},{5,4},{6,5},{7,6},{9,8},{10,9},{11,10},{12... | collective-permute-start | bytes 6266888 | tf_op jit(solution)/shard_map/ppermute | solution.py:12
  83.9 62.6 %all-to-all-start = ((bf16[2,512,16,128]{3,2,0,1:T(8,128)(2,1)}), bf16[2,512,16,128]{3,2,0,1:T(8,128)(2,1)}, u32[]{:S(2)}, u32[]{:S(2)}) async-start(bf16[2,512,16,128]{3,2,0,1:T(8,128)(2,1)} %copy.24), calls=%async_computation | async-start | bytes 8388608 | tf_op jit(solution)/shard_map/all_to_all | solution.py:72
where the time goes:
time: 239 us; the launch traced here: 238 us
  waiting for transfers between devices  98.3 us (41%)
  blocking collectives  68.4 us (29%)
  local copies, waits for them, and re-layouts  33.6 us (14%)
  matrix products  24 us (10%)
  starting transfers between devices  7.05 us (3%)
  other arithmetic  6.41 us (3%)
    all_to_all x1, blocking collectives, per_device(): lax.all_to_all(spectrum, ('pa', 'row'), split_axis=2, concat_axis=1, tile...  68.4 us
    all_to_all x1, waiting for transfers between devices, per_device(): lax.all_to_all(compressed, 'pa', split_axis=1, concat_axis=2, tiled=True)  54.6 us
    ppermute x1, waiting for transfers between devices, shifted(): return lax.ppermute(array, axis, pairs)  43.7 us
    dot_general x1, matrix products, per_device(): jnp.dot(banded, flattened, preferred_element_type=jnp.float32)  17.8 us
    convert_element_type x1, local copies, waits for them, and re-layouts, per_device(): spectrum = jnp.einsum('xbyp,ygpe->xgbe', matrix, turned, preferred_elemen...  11.2 us
    unnamed x3, local copies, waits for them, and re-layouts  5.95 us
    all_to_all x1, starting transfers between devices, per_device(): lax.all_to_all(compressed, 'pa', split_axis=1, concat_axis=2, tiled=True)  5.77 us
  transfers between devices with their start and end apart: 2, of which 2 were waited for; matrix products, arithmetic and copies ran while one was open for 3% of the time, Pallas kernels for 0%

commit v1 on v0

v1 whole, which is shorter than its diff:
```python
import functools
import math

import jax
import jax.numpy as jnp
import numpy as np
from jax import lax
from jax.experimental import pallas as pl
from jax.experimental.pallas import tpu as pltpu
from jax.sharding import PartitionSpec as P


def filter_parts(chirp_phase):
    scaling = 1.0 / math.sqrt(chirp_phase.shape[0])
    real_part = (jnp.cos(chirp_phase) * scaling).astype(jnp.bfloat16)
    imag_part = (-jnp.sin(chirp_phase) * scaling).astype(jnp.bfloat16)
    return (real_part, imag_part)


def doppler_matrix(pulses):
    indices = np.arange(pulses)
    products = indices[:, None] * indices[None, :] % pulses
    angles = (np.float32(2.0 * math.pi / pulses) * products.astype(np.float32)).astype(np.float64)
    scaling = 1.0 / math.sqrt(pulses)
    real_part = (np.cos(angles) * scaling).astype(np.float32)
    imag_part = (-np.sin(angles) * scaling).astype(np.float32)
    upper_half = np.stack([real_part, -imag_part], axis=1)
    lower_half = np.stack([imag_part, real_part], axis=1)
    matrix = np.stack([upper_half, lower_half], axis=1)
    return matrix.reshape(2 * pulses, 2 * pulses).astype(jnp.bfloat16)


def doppler_kernel(matrix_ref, samples_ref, out_ref, scratch):
    rows = matrix_ref.shape[0]
    gates, element_count = out_ref.shape[1:]
    matrix = matrix_ref[...]

    def columns(gate):
        parts = [samples_ref[:, part, gate].reshape(-1, element_count) for part in range(2)]
        return jnp.concatenate(parts, axis=0)

    for gate in range(0, gates, 2):
        both = jnp.concatenate([columns(gate), columns(gate + 1)], axis=1)
        product = jnp.dot(matrix, both, preferred_element_type=jnp.float32)
        for k in range(2):
            scratch[gate + k] = product[:, k * element_count : (k + 1) * element_count]
    step = 32
    for row in range(0, rows, step):
        block = scratch[:, row : row + step, :]
        out_ref[row : row + step] = jnp.transpose(block, (1, 0, 2)).astype(jnp.bfloat16)


def doppler(matrix, samples):
    owners, _, gates, pulses_dev, element_count = samples.shape
    rows = matrix.shape[0]
    block = math.gcd(16, gates)
    return pl.pallas_call(
        doppler_kernel,
        out_shape=jax.ShapeDtypeStruct((rows, gates, element_count), jnp.bfloat16),
        grid=(gates // block,),
        in_specs=[
            pl.BlockSpec(matrix.shape, lambda i: (0, 0)),
            pl.BlockSpec(
                (owners, 2, block, pulses_dev, element_count), lambda i: (0, 0, i, 0, 0)
            ),
        ],
        out_specs=pl.BlockSpec((rows, block, element_count), lambda i: (0, i, 0)),
        scratch_shapes=[pltpu.VMEM((block, rows, element_count), jnp.float32)],
        compiler_params=pltpu.CompilerParams(vmem_limit_bytes=48 << 20),
        name="doppler",
    )(matrix, samples)


def covariance_kernel(total_gates, taps_ref, samples_ref, out_ref):
    pa_count, row_count, bins, _, gates, element_count = samples_ref.shape
    tile = taps_ref.shape[1] // 2
    owners = tile // gates
    tiles_row = pa_count // owners

    def band(part):
        values = jnp.broadcast_to(taps_ref[part : part + 1, :], (tile, 2 * tile))
        return pltpu.roll(values, 0, 1, stride=1, stride_axis=0).astype(jnp.bfloat16)

    real_band, imag_band = band(0), band(1)
    own = jnp.concatenate([real_band[:, :tile], imag_band[:, :tile]], axis=1)
    before = jnp.concatenate([real_band[:, tile:], imag_band[:, tile:]], axis=1)
    bands = jnp.concatenate([own, before], axis=0)
    for b in range(bins):
        gram = jnp.zeros((2 * element_count, 2 * element_count), jnp.float32)
        carried = None
        for t in reversed(range(row_count * tiles_row)):
            row, first = t // tiles_row, t % tiles_row * owners
            real, imag = (
                samples_ref[first : first + owners, row, b, part].reshape(tile, element_count)
                for part in range(2)
            )
            upper = jnp.concatenate([real, imag], axis=1)
            lower = jnp.concatenate([-imag, real], axis=1)
            both = jnp.concatenate([upper, lower], axis=0)
            product = jnp.dot(bands, both, preferred_element_type=jnp.float32)
            filtered = product[:tile] if carried is None else product[:tile] + carried
            carried = product[tile:]
            filtered = filtered.astype(jnp.bfloat16)
            gram = gram + lax.dot_general(
                filtered, filtered, (((0,), (0,)), ((), ())), preferred_element_type=jnp.float32
            )
        n = element_count
        out_ref[b, 0] = (gram[:n, :n] + gram[n:, n:]) / total_gates
        out_ref[b, 1] = (gram[n:, :n] - gram[:n, n:]) / total_gates


def covariances(taps, samples, total_gates):
    bins, element_count = samples.shape[2], samples.shape[-1]
    return pl.pallas_call(
        functools.partial(covariance_kernel, total_gates),
        out_shape=jax.ShapeDtypeStruct((bins, 2, element_count, element_count), jnp.float32),
        in_specs=[pl.BlockSpec(memory_space=pltpu.VMEM)] * 2,
        out_specs=pl.BlockSpec(memory_space=pltpu.VMEM),
        compiler_params=pltpu.CompilerParams(vmem_limit_bytes=48 << 20),
        name="covariances",
    )(taps, samples)


def per_device(echoes, chirp_phase):
    gates_dev, pulses_dev, element_count = echoes.shape[1:]
    tap_count = chirp_phase.shape[0]
    pa_count, row_count = lax.axis_size("pa"), lax.axis_size("row")
    pulses, total_gates = pulses_dev * pa_count, gates_dev * row_count
    devices = pa_count * row_count
    gates = gates_dev // pa_count
    bins = pulses // devices
    taps = jnp.stack(filter_parts(chirp_phase)).astype(jnp.float32)
    taps = jnp.pad(taps, ((0, 0), (0, tap_count)))
    blocks = echoes.reshape(2, pa_count, gates, pulses_dev, element_count).swapaxes(0, 1)
    turned = lax.all_to_all(blocks, "pa", split_axis=0, concat_axis=0, tiled=True)
    spectrum = doppler(jnp.asarray(doppler_matrix(pulses)), turned)
    spectrum = spectrum.reshape(devices, bins, 2, gates, element_count)
    owned = lax.all_to_all(spectrum, ("pa", "row"), split_axis=0, concat_axis=0, tiled=True)
    owned = owned.reshape(pa_count, row_count, bins, 2, gates, element_count)
    return covariances(taps, owned, total_gates)


def solution(mesh):
    placed = (P(None, "row", "pa", None), P())
    return jax.shard_map(
        per_device,
        mesh=mesh,
        in_specs=placed,
        out_specs=P(("pa", "row"), None, None, None),
        check_vma=False,
    )
```

time: 239 us -> 141 us (0.59)
  waiting for transfers between devices: 98.3 us -> 51.4 us
  local copies, waits for them, and re-layouts: 33.6 us -> 4.9 us
  matrix products: 24 us -> 0 us
  Pallas kernels: 0 us -> 19.6 us
  blocking collectives: 68.4 us -> 55.8 us
  other arithmetic: 6.41 us -> 0.05 us
    ppermute x1 -> x0, waiting for transfers between devices: 43.7 us -> none  [shifted(): return lax.ppermute(array, axis, pairs)]
    dot_general x3 -> x0, matrix products: 24 us -> none  [the longest x1 17.8 us: per_device(): jnp.dot(banded, flattened, preferred_element_type=jnp.float32)]
    pallas_call x0 -> x2, Pallas kernels: none -> 19.6 us  [the longest x1 13.9 us: covariances(): pl.pallas_call(functools.partial(covariance_kernel, total_gates), out_sha...]
    all_to_all x1, blocking collectives: 68.4 us -> 55.8 us  [per_device(): lax.all_to_all(blocks, 'pa', split_axis=0, concat_axis=0, tiled=True)]
    convert_element_type x1 -> x0, local copies, waits for them, and re-layouts: 11.2 us -> none  [per_device(): spectrum = jnp.einsum('xbyp,ygpe->xgbe', matrix, turned, preferred_elemen...]
    all_to_all x3 -> x0, local copies, waits for them, and re-layouts: 4.85 us -> none  [the longest x1 3.4 us: per_device(): lax.all_to_all(compressed, 'pa', split_axis=1, concat_axis=2, tiled=True)]
    unnamed x3 -> x6, local copies, waits for them, and re-layouts: 5.95 us -> 1.98 us
    concatenate x1 -> x0, other arithmetic: 3.36 us -> none  [per_device(): extended = jnp.concatenate([echoes, following], axis=1)]
  transfers between devices with their start and end apart: 2 -> 1, of which waited for: 2 -> 1; matrix products, arithmetic and copies ran while one was open for 3% -> 0% of each run, Pallas kernels for 0% -> 0%
where the time goes in v1:
time: 141 us
  blocking collectives  55.8 us (40%)
  waiting for transfers between devices  51.4 us (36%)
  Pallas kernels  19.6 us (14%)
  starting transfers between devices  9 us (6%)
  local copies, waits for them, and re-layouts  4.9 us (3%)
    all_to_all x1, blocking collectives, per_device(): lax.all_to_all(blocks, 'pa', split_axis=0, concat_axis=0, tiled=True)  55.8 us
    all_to_all x1, waiting for transfers between devices, per_device(): lax.all_to_all(spectrum, ('pa', 'row'), split_axis=0, concat_axis=0, tile...  51.4 us
    pallas_call x1, Pallas kernels, covariances(): pl.pallas_call(functools.partial(covariance_kernel, total_gates), out_sha...  13.9 us
    all_to_all x1, starting transfers between devices, per_device(): lax.all_to_all(spectrum, ('pa', 'row'), split_axis=0, concat_axis=0, tile...  9 us
    pallas_call x1, Pallas kernels, doppler(): pl.pallas_call(doppler_kernel, out_shape=jax.ShapeDtypeStruct((rows, gate...  5.76 us
    reshape x1, local copies, waits for them, and re-layouts, per_device(): echoes.reshape(2, pa_count, gates, pulses_dev, element_count).swapaxes(0, 1)  2.91 us
  transfers between devices with their start and end apart: 1, of which 1 were waited for; matrix products, arithmetic and copies ran while one was open for 0% of the time, Pallas kernels for 0%

profile of v1, /device:TPU:0, one launch (start us, length us, event | category | flops | bytes accessed | tf_op | source)
XLA Modules:
  0.0 140.9 jit_solution(14577671663337727280)
XLA Ops:
  0.0 2.9 %copy.6 = bf16[2,16,32,16,128]{4,3,2,0,1:T(8,128)(2,1)S(1)} copy(bf16[2,16,32,16,128]{4,3,2,1,0:T(8,128)(2,1)} %bitcast.8) | data formatting | bytes 8388608 | tf_op jit(solution)/shard_map/reshape | solution.py:134
  2.9 0.0 copy-start.1
  2.9 55.8 %all_to_all.10.samples_ref = bf16[16,2,32,16,128]{4,3,2,1,0:T(8,128)(2,1)} all-to-all(bf16[16,2,32,16,128]{4,3,2,1,0:T(8,128)(2,1)S(1)} %bitcast.7), channel_id=1, replica_groups=mesh['pa'=16,'row'=8] {'pa'}, dimensions={0} | all-to-all | bytes 8388608 | tf_op jit(solution)/shard_map/all_to_all | solution.py:135
  58.7 0.0 copy-done.1
  58.7 5.8 %doppler.1 = bf16[512,32,128]{2,1,0:T(8,128)(2,1)S(1)} custom-call(bf16[512,512]{1,0:T(8,128)(2,1)S(1)} %copy-done.1, bf16[16,2,32,16,128]{4,3,2,1,0:T(8,128)(2,1)} %all_to_all.10.samples_ref), custom_call_target="tpu_custom_call" | custom-call | tf_op jit(solution)/shard_map/doppler/pallas_call | solution.py:57
  64.5 0.0 copy-start
  64.5 2.0 %copy-done = bf16[512,32,128]{2,1,0:T(8,128)(2,1)} copy-done((bf16[512,32,128]{2,1,0:T(8,128)(2,1)}, bf16[512,32,128]{2,1,0:T(8,128)(2,1)S(1)}, u32[]{:S(2)}) %copy-start) | copy-done | bytes 4194328
  66.5 0.0 copy-start.2
  66.5 9.0 %all-to-all-start.1 = ((bf16[128,2,2,32,128]{4,3,2,1,0:T(8,128)(2,1)}), bf16[128,2,2,32,128]{4,3,2,1,0:T(8,128)(2,1)}, u32[]{:S(2)}, u32[]{:S(2)}) async-start(bf16[128,2,2,32,128]{4,3,2,1,0:T(8,128)(2,1)} %bitcast.6), calls=%async_computation.1 | async-start | bytes 8388608 | tf_op jit(solution)/shard_map/all_to_all | solution.py:138
  75.5 0.0 copy-done.2
  75.6 51.4 %all-to-all-done.1 = bf16[128,2,2,32,128]{4,3,2,1,0:T(8,128)(2,1)} async-done(((bf16[128,2,2,32,128]{4,3,2,1,0:T(8,128)(2,1)}), bf16[128,2,2,32,128]{4,3,2,1,0:T(8,128)(2,1)}, u32[]{:S(2)}, u32[]{:S(2)}) %all-to-all-start.1) | async-done | bytes 4194336 | tf_op jit(solution)/shard_map/all_to_all | solution.py:138
  127.0 13.9 %covariances.1 = f32[2,2,128,128]{3,2,1,0:T(8,128)} custom-call(f32[2,512]{1,0:T(2,128)S(1)} %fusion.3.taps_ref, bf16[16,8,2,2,32,128]{5,4,3,2,1,0:T(8,128)(2,1)} %bitcast.3.samples_ref), custom_call_target="tpu_custom_call" | custom-call | tf_op jit(solution)/shard_map/covariances/pallas_call | solution.py:114
  (4 shorter events, 0.1 us)
Async XLA Ops:
  2.9 55.8 %copy-start.1 = (bf16[512,512]{1,0:T(8,128)(2,1)S(1)}, bf16[512,512]{1,0:T(8,128)(2,1)}, u32[]{:S(2)}) copy-start(bf16[512,512]{1,0:T(8,128)(2,1)} %constant.8.clone.matrix_ref) | copy-start | bytes 1572868
  64.5 2.0 %copy-start = (bf16[512,32,128]{2,1,0:T(8,128)(2,1)}, bf16[512,32,128]{2,1,0:T(8,128)(2,1)S(1)}, u32[]{:S(2)}) copy-start(bf16[512,32,128]{2,1,0:T(8,128)(2,1)S(1)} %doppler.1) | copy-start | bytes 12582916
  66.5 9.0 %copy-start.2 = (f32[256]{0:T(256)S(1)}, f32[256]{0:T(256)}, u32[]{:S(2)}) copy-start(f32[256]{0:T(256)} %param.4) | copy-start | bytes 3076
  66.5 60.5 %all-to-all-start.1 = ((bf16[128,2,2,32,128]{4,3,2,1,0:T(8,128)(2,1)}), bf16[128,2,2,32,128]{4,3,2,1,0:T(8,128)(2,1)}, u32[]{:S(2)}, u32[]{:S(2)}) async-start(bf16[128,2,2,32,128]{4,3,2,1,0:T(8,128)(2,1)} %bitcast.6), calls=%async_computation.1 | async-start | bytes 8388608 | tf_op jit(solution)/shard_map/all_to_all | solution.py:138

commit v2 on v1

v2 whole, which is shorter than its diff:
```python
import functools
import math

import jax
import jax.numpy as jnp
import numpy as np
from jax import lax
from jax.experimental import pallas as pl
from jax.experimental.pallas import tpu as pltpu
from jax.sharding import PartitionSpec as P


def doppler_matrix(pulses):
    indices = np.arange(pulses)
    products = indices[:, None] * indices[None, :] % pulses
    angles = (np.float32(2.0 * math.pi / pulses) * products.astype(np.float32)).astype(np.float64)
    scaling = 1.0 / math.sqrt(pulses)
    real_part = (np.cos(angles) * scaling).astype(np.float32)
    imag_part = (-np.sin(angles) * scaling).astype(np.float32)
    upper_half = np.stack([real_part, -imag_part], axis=1)
    lower_half = np.stack([imag_part, real_part], axis=1)
    matrix = np.stack([upper_half, lower_half], axis=1)
    return matrix.reshape(2 * pulses, 2 * pulses).astype(jnp.bfloat16)


def doppler_kernel(matrix_ref, samples_ref, out_ref, scratch):
    rows = matrix_ref.shape[0]
    gates, element_count = out_ref.shape[1:]
    matrix = matrix_ref[...]

    def columns(gate):
        parts = [samples_ref[:, part, gate].reshape(-1, element_count) for part in range(2)]
        return jnp.concatenate(parts, axis=0)

    for gate in range(0, gates, 2):
        both = jnp.concatenate([columns(gate), columns(gate + 1)], axis=1)
        product = jnp.dot(matrix, both, preferred_element_type=jnp.float32)
        for k in range(2):
            scratch[gate + k] = product[:, k * element_count : (k + 1) * element_count]
    step = 32
    for row in range(0, rows, step):
        block = scratch[:, row : row + step, :]
        out_ref[row : row + step] = jnp.transpose(block, (1, 0, 2)).astype(jnp.bfloat16)


def doppler(matrix, samples):
    owners, _, gates, pulses_dev, element_count = samples.shape
    rows = matrix.shape[0]
    block = math.gcd(16, gates)
    return pl.pallas_call(
        doppler_kernel,
        out_shape=jax.ShapeDtypeStruct((rows, gates, element_count), jnp.bfloat16),
        grid=(gates // block,),
        in_specs=[
            pl.BlockSpec(matrix.shape, lambda i: (0, 0)),
            pl.BlockSpec(
                (owners, 2, block, pulses_dev, element_count), lambda i: (0, 0, i, 0, 0)
            ),
        ],
        out_specs=pl.BlockSpec((rows, block, element_count), lambda i: (0, i, 0)),
        scratch_shapes=[pltpu.VMEM((block, rows, element_count), jnp.float32)],
        compiler_params=pltpu.CompilerParams(vmem_limit_bytes=20 << 20),
        name="doppler",
    )(matrix, samples)


def covariance_kernel(total_gates, phase_ref, samples_ref, out_ref):
    pa_count, row_count, _, _, gates, element_count = samples_ref.shape
    tile = phase_ref.shape[1]
    owners = tile // gates
    tiles_row = pa_count // owners
    scaling = 1.0 / math.sqrt(tile)

    def band(values):
        values = (values * scaling).astype(jnp.bfloat16).astype(jnp.float32)
        values = jnp.concatenate([values, jnp.zeros_like(values)], axis=1)
        values = jnp.broadcast_to(values, (tile, 2 * tile))
        return pltpu.roll(values, 0, 1, stride=1, stride_axis=0).astype(jnp.bfloat16)

    real_band, imag_band = band(jnp.cos(phase_ref[...])), band(-jnp.sin(phase_ref[...]))
    own = jnp.concatenate([real_band[:, :tile], imag_band[:, :tile]], axis=1)
    before = jnp.concatenate([real_band[:, tile:], imag_band[:, tile:]], axis=1)
    bands = jnp.concatenate([own, before], axis=0)
    n = element_count
    gram = jnp.zeros((2 * n, 2 * n), jnp.float32)
    carried = None
    for t in reversed(range(row_count * tiles_row)):
        row, first = t // tiles_row, t % tiles_row * owners
        real, imag = (
            samples_ref[first : first + owners, row, 0, part].reshape(tile, n) for part in range(2)
        )
        upper = jnp.concatenate([real, imag], axis=1)
        lower = jnp.concatenate([-imag, real], axis=1)
        both = jnp.concatenate([upper, lower], axis=0)
        product = jnp.dot(bands, both, preferred_element_type=jnp.float32)
        filtered = product[:tile] if carried is None else product[:tile] + carried
        carried = product[tile:]
        filtered = filtered.astype(jnp.bfloat16)
        gram = gram + lax.dot_general(
            filtered, filtered, (((0,), (0,)), ((), ())), preferred_element_type=jnp.float32
        )
    out_ref[0, 0] = (gram[:n, :n] + gram[n:, n:]) / total_gates
    out_ref[0, 1] = (gram[n:, :n] - gram[:n, n:]) / total_gates


def covariances(phase, samples, total_gates):
    pa_count, row_count, bins, _, gates, element_count = samples.shape
    return pl.pallas_call(
        functools.partial(covariance_kernel, total_gates),
        out_shape=jax.ShapeDtypeStruct((bins, 2, element_count, element_count), jnp.float32),
        grid=(bins,),
        in_specs=[
            pl.BlockSpec(phase.shape, lambda b: (0, 0)),
            pl.BlockSpec(
                (pa_count, row_count, 1, 2, gates, element_count), lambda b: (0, 0, b, 0, 0, 0)
            ),
        ],
        out_specs=pl.BlockSpec((1, 2, element_count, element_count), lambda b: (b, 0, 0, 0)),
        compiler_params=pltpu.CompilerParams(vmem_limit_bytes=20 << 20),
        name="covariances",
    )(phase, samples)


def per_device(echoes, chirp_phase):
    gates_dev, pulses_dev, element_count = echoes.shape[1:]
    pa_count, row_count = lax.axis_size("pa"), lax.axis_size("row")
    pulses, total_gates = pulses_dev * pa_count, gates_dev * row_count
    devices = pa_count * row_count
    gates = gates_dev // pa_count
    bins = pulses // devices
    blocks = echoes.reshape(2, pa_count, gates, pulses_dev, element_count).swapaxes(0, 1)
    turned = lax.all_to_all(blocks, "pa", split_axis=0, concat_axis=0, tiled=True)
    spectrum = doppler(jnp.asarray(doppler_matrix(pulses)), turned)
    spectrum = spectrum.reshape(devices, bins, 2, gates, element_count)
    owned = lax.all_to_all(spectrum, ("pa", "row"), split_axis=0, concat_axis=0, tiled=True)
    owned = owned.reshape(pa_count, row_count, bins, 2, gates, element_count)
    return covariances(chirp_phase[None], owned, total_gates)


def solution(mesh):
    placed = (P(None, "row", "pa", None), P())
    return jax.shard_map(
        per_device,
        mesh=mesh,
        in_specs=placed,
        out_specs=P(("pa", "row"), None, None, None),
        check_vma=False,
    )
```

time: 141 us -> 131 us (0.929)
  blocking collectives: 55.8 us -> 116 us
  waiting for transfers between devices: 51.4 us -> 0 us
  starting transfers between devices: 9 us -> 0 us
  Pallas kernels: 19.6 us -> 12.2 us
  local copies, waits for them, and re-layouts: 4.9 us -> 2.92 us
    all_to_all x0 -> x1, blocking collectives: none -> 60.2 us  [per_device(): lax.all_to_all(spectrum, ('pa', 'row'), split_axis=0, concat_axis=0, tile...]
    all_to_all x1 -> x0, waiting for transfers between devices: 51.4 us -> none  [per_device(): lax.all_to_all(spectrum, ('pa', 'row'), split_axis=0, concat_axis=0, tile...]
    all_to_all x1 -> x0, starting transfers between devices: 9 us -> none  [per_device(): lax.all_to_all(spectrum, ('pa', 'row'), split_axis=0, concat_axis=0, tile...]
    pallas_call x1, Pallas kernels: 13.9 us -> 7.77 us  [covariances(): pl.pallas_call(functools.partial(covariance_kernel, total_gates), out_sha...]
    unnamed x6 -> x4, local copies, waits for them, and re-layouts: 1.98 us -> 0.01 us
  transfers between devices with their start and end apart: 1 -> 0, of which waited for: 1 -> 0; matrix products, arithmetic and copies ran while one was open for 0% -> 0% of each run, Pallas kernels for 0% -> 0%
where the time goes in v2:
time: 131 us
  blocking collectives  116 us (89%)
  Pallas kernels  12.2 us (9%)
  local copies, waits for them, and re-layouts  2.92 us (2%)
    all_to_all x1, blocking collectives, per_device(): lax.all_to_all(spectrum, ('pa', 'row'), split_axis=0, concat_axis=0, tile...  60.2 us
    all_to_all x1, blocking collectives, per_device(): lax.all_to_all(blocks, 'pa', split_axis=0, concat_axis=0, tiled=True)  55.7 us
    pallas_call x1, Pallas kernels, covariances(): pl.pallas_call(functools.partial(covariance_kernel, total_gates), out_sha...  7.77 us
    pallas_call x1, Pallas kernels, doppler(): pl.pallas_call(doppler_kernel, out_shape=jax.ShapeDtypeStruct((rows, gate...  4.44 us
    reshape x1, local copies, waits for them, and re-layouts, per_device(): echoes.reshape(2, pa_count, gates, pulses_dev, element_count).swapaxes(0, 1)  2.91 us

profile of v2, /device:TPU:0, one launch (start us, length us, event | category | flops | bytes accessed | tf_op | source)
XLA Modules:
  0.0 131.1 jit_solution(9534370760604293839)
XLA Ops:
  0.0 2.9 %copy.6 = bf16[2,16,32,16,128]{4,3,2,0,1:T(8,128)(2,1)S(1)} copy(bf16[2,16,32,16,128]{4,3,2,1,0:T(8,128)(2,1)} %bitcast.11) | data formatting | bytes 8388608 | tf_op jit(solution)/shard_map/reshape | solution.py:131
  2.9 0.0 copy-start
  2.9 55.7 %all_to_all.10.samples_ref = bf16[16,2,32,16,128]{4,3,2,1,0:T(8,128)(2,1)S(1)} all-to-all(bf16[16,2,32,16,128]{4,3,2,1,0:T(8,128)(2,1)S(1)} %bitcast.10), channel_id=1, replica_groups=mesh['pa'=16,'row'=8] {'pa'}, dimensions={0} | all-to-all | bytes 8388608 | tf_op jit(solution)/shard_map/all_to_all | solution.py:132
  58.6 0.0 copy-done
  58.6 4.4 %doppler.1 = bf16[512,32,128]{2,1,0:T(8,128)(2,1)S(1)} custom-call(bf16[512,512]{1,0:T(8,128)(2,1)S(1)} %copy-done, bf16[16,2,32,16,128]{4,3,2,1,0:T(8,128)(2,1)S(1)} %all_to_all.10.samples_ref), custom_call_target="tpu_custom_call" | custom-call | tf_op jit(solution)/shard_map/doppler/pallas_call | solution.py:50
  63.1 0.0 copy-start.1
  63.1 60.2 %all_to_all.11 = bf16[128,2,2,32,128]{4,3,2,1,0:T(8,128)(2,1)S(1)} all-to-all(bf16[128,2,2,32,128]{4,3,2,1,0:T(8,128)(2,1)S(1)} %bitcast.7), channel_id=1, replica_groups=mesh['pa'=16,'row'=8] {'pa','row'}, dimensions={0} | all-to-all | bytes 8388608 | tf_op jit(solution)/shard_map/all_to_all | solution.py:135
  123.3 0.0 copy-done.1
  123.3 7.8 %covariances.1 = f32[2,2,128,128]{3,2,1,0:T(8,128)} custom-call(f32[1,256]{1,0:T(1,128)S(1)} %bitcast.9, bf16[16,8,2,2,32,128]{5,4,3,2,1,0:T(8,128)(2,1)S(1)} %bitcast.8), custom_call_target="tpu_custom_call" | custom-call | tf_op jit(solution)/shard_map/covariances/pallas_call | solution.py:108
Async XLA Ops:
  2.9 55.7 %copy-start = (bf16[512,512]{1,0:T(8,128)(2,1)S(1)}, bf16[512,512]{1,0:T(8,128)(2,1)}, u32[]{:S(2)}) copy-start(bf16[512,512]{1,0:T(8,128)(2,1)} %constant.2.clone.matrix_ref) | copy-start | bytes 1572868
  63.1 60.3 %copy-start.1 = (f32[256]{0:T(256)S(1)}, f32[256]{0:T(256)}, u32[]{:S(2)}) copy-start(f32[256]{0:T(256)} %param.4) | copy-start | bytes 3076

commit v3 on v2

v3 whole, which is shorter than its diff:
```python
import functools
import math

import jax
import jax.numpy as jnp
import numpy as np
from jax import lax
from jax.experimental import pallas as pl
from jax.experimental.pallas import tpu as pltpu
from jax.sharding import PartitionSpec as P


def doppler_matrix(pulses):
    indices = np.arange(pulses)
    products = indices[:, None] * indices[None, :] % pulses
    angles = (np.float32(2.0 * math.pi / pulses) * products.astype(np.float32)).astype(np.float64)
    scaling = 1.0 / math.sqrt(pulses)
    real_part = (np.cos(angles) * scaling).astype(np.float32)
    imag_part = (-np.sin(angles) * scaling).astype(np.float32)
    upper_half = np.stack([real_part, -imag_part], axis=1)
    lower_half = np.stack([imag_part, real_part], axis=1)
    matrix = np.stack([upper_half, lower_half], axis=1)
    return matrix.reshape(2 * pulses, 2 * pulses).astype(jnp.bfloat16)


def doppler_kernel(matrix_ref, samples_ref, out_ref, scratch):
    rows = matrix_ref.shape[0]
    gates, element_count = out_ref.shape[1:]
    slots, group = scratch.shape[:2]

    def columns(gate):
        parts = [samples_ref[:, part, gate].reshape(-1, element_count) for part in range(2)]
        return jnp.concatenate(parts, axis=0)

    step = 32
    for first in range(0, gates, group):
        slot = first // group % slots
        for k in range(0, group, 2):
            both = jnp.concatenate([columns(first + k), columns(first + k + 1)], axis=1)
            product = jnp.dot(matrix_ref[...], both, preferred_element_type=jnp.float32)
            scratch[slot, k] = product[:, :element_count]
            scratch[slot, k + 1] = product[:, element_count:]
        for row in range(0, rows, step):
            block = jnp.transpose(scratch[slot, :, row : row + step, :], (1, 0, 2))
            out_ref[row : row + step, first : first + group] = block.astype(jnp.bfloat16)


def doppler(matrix, samples):
    gates, _, element_count = samples.shape[2:]
    rows = matrix.shape[0]
    group = math.gcd(16, gates)
    return pl.pallas_call(
        doppler_kernel,
        out_shape=jax.ShapeDtypeStruct((rows, gates, element_count), jnp.bfloat16),
        in_specs=[pl.BlockSpec(memory_space=pltpu.VMEM)] * 2,
        out_specs=pl.BlockSpec(memory_space=pltpu.VMEM),
        scratch_shapes=[pltpu.VMEM((2, group, rows, element_count), jnp.float32)],
        compiler_params=pltpu.CompilerParams(vmem_limit_bytes=24 << 20),
        name="doppler",
    )(matrix, samples)


def covariance_kernel(total_gates, phase_ref, samples_ref, out_ref):
    pa_count, row_count, _, _, gates, n = samples_ref.shape
    b = pl.program_id(0)
    taps = phase_ref.shape[1]
    reach = 2
    tile = taps // reach
    owners = tile // gates
    tiles_row = pa_count // owners
    scaling = 1.0 / math.sqrt(taps)

    def band(values):
        values = (values * scaling).astype(jnp.bfloat16).astype(jnp.float32)
        values = jnp.concatenate([values, jnp.zeros((1, tile), jnp.float32)], axis=1)
        values = jnp.broadcast_to(values, (tile, taps + tile))
        return pltpu.roll(values, 0, 1, stride=1, stride_axis=0).astype(jnp.bfloat16)

    real_band, imag_band = band(jnp.cos(phase_ref[...])), band(-jnp.sin(phase_ref[...]))
    parts = [slice(k * tile, (k + 1) * tile) for k in range(reach + 1)]
    bands = [jnp.concatenate([real_band[:, k], imag_band[:, k]], axis=1) for k in parts]
    bands = jnp.concatenate(bands, axis=0)
    gram = jnp.zeros((2 * n, 2 * n), jnp.float32)
    carried = [None] * reach
    waiting = []
    for t in reversed(range(row_count * tiles_row)):
        row, first = t // tiles_row, t % tiles_row * owners
        real, imag = (
            samples_ref[first : first + owners, row, b, part].reshape(tile, n) for part in range(2)
        )
        upper = jnp.concatenate([real, imag], axis=1)
        lower = jnp.concatenate([-imag, real], axis=1)
        both = jnp.concatenate([upper, lower], axis=0)
        product = jnp.dot(bands, both, preferred_element_type=jnp.float32)
        sums = [product[k] for k in parts]
        sums = [x if y is None else x + y for x, y in zip(sums, carried + [None])]
        carried = sums[1:]
        waiting.append(sums[0].astype(jnp.bfloat16))
        if len(waiting) == reach:
            filtered = jnp.concatenate(waiting, axis=0)
            waiting = []
            gram = gram + lax.dot_general(
                filtered, filtered, (((0,), (0,)), ((), ())), preferred_element_type=jnp.float32
            )
    out_ref[0, 0] = (gram[:n, :n] + gram[n:, n:]) / total_gates
    out_ref[0, 1] = (gram[n:, :n] - gram[:n, n:]) / total_gates


def covariances(phase, samples, total_gates):
    bins, element_count = samples.shape[2], samples.shape[-1]
    return pl.pallas_call(
        functools.partial(covariance_kernel, total_gates),
        out_shape=jax.ShapeDtypeStruct((bins, 2, element_count, element_count), jnp.float32),
        grid=(bins,),
        in_specs=[pl.BlockSpec(memory_space=pltpu.VMEM)] * 2,
        out_specs=pl.BlockSpec((1, 2, element_count, element_count), lambda b: (b, 0, 0, 0)),
        compiler_params=pltpu.CompilerParams(vmem_limit_bytes=20 << 20),
        name="covariances",
    )(phase, samples)


def per_device(echoes, chirp_phase):
    gates_dev, pulses_dev, element_count = echoes.shape[1:]
    pa_count, row_count = lax.axis_size("pa"), lax.axis_size("row")
    pulses, total_gates = pulses_dev * pa_count, gates_dev * row_count
    devices = pa_count * row_count
    gates = gates_dev // pa_count
    bins = pulses // devices
    blocks = echoes.reshape(2, pa_count, gates, pulses_dev, element_count).swapaxes(0, 1)
    turned = lax.all_to_all(blocks, "pa", split_axis=0, concat_axis=0, tiled=True)
    spectrum = doppler(jnp.asarray(doppler_matrix(pulses)), turned)
    spectrum = spectrum.reshape(devices, bins, 2, gates, element_count)
    owned = lax.all_to_all(spectrum, ("pa", "row"), split_axis=0, concat_axis=0, tiled=True)
    owned = owned.reshape(pa_count, row_count, bins, 2, gates, element_count)
    return covariances(chirp_phase[None], owned, total_gates)


def solution(mesh):
    placed = (P(None, "row", "pa", None), P())
    return jax.shard_map(
        per_device,
        mesh=mesh,
        in_specs=placed,
        out_specs=P(("pa", "row"), None, None, None),
        check_vma=False,
    )
```

time: 131 us -> 129 us (0.985)
  Pallas kernels: 12.2 us -> 9.65 us
where the time goes in v3:
time: 129 us
  blocking collectives  116 us (90%)
  Pallas kernels  9.65 us (7%)
  local copies, waits for them, and re-layouts  2.92 us (2%)
    all_to_all x1, blocking collectives, per_device(): lax.all_to_all(spectrum, ('pa', 'row'), split_axis=0, concat_axis=0, tile...  60.2 us
    all_to_all x1, blocking collectives, per_device(): lax.all_to_all(blocks, 'pa', split_axis=0, concat_axis=0, tiled=True)  55.7 us
    pallas_call x1, Pallas kernels, covariances(): pl.pallas_call(functools.partial(covariance_kernel, total_gates), out_sha...  6.47 us
    pallas_call x1, Pallas kernels, doppler(): pl.pallas_call(doppler_kernel, out_shape=jax.ShapeDtypeStruct((rows, gate...  3.18 us
    reshape x1, local copies, waits for them, and re-layouts, per_device(): echoes.reshape(2, pa_count, gates, pulses_dev, element_count).swapaxes(0, 1)  2.91 us

profile of v3, /device:TPU:0, one launch (start us, length us, event | category | flops | bytes accessed | tf_op | source)
XLA Modules:
  0.0 128.5 jit_solution(6662114402443704348)
XLA Ops:
  0.0 2.9 %copy.6 = bf16[2,16,32,16,128]{4,3,2,0,1:T(8,128)(2,1)S(1)} copy(bf16[2,16,32,16,128]{4,3,2,1,0:T(8,128)(2,1)} %bitcast.11) | data formatting | bytes 8388608 | tf_op jit(solution)/shard_map/reshape | solution.py:129
  2.9 0.0 copy-start
  2.9 55.7 %all_to_all.10.samples_ref = bf16[16,2,32,16,128]{4,3,2,1,0:T(8,128)(2,1)S(1)} all-to-all(bf16[16,2,32,16,128]{4,3,2,1,0:T(8,128)(2,1)S(1)} %bitcast.10), channel_id=1, replica_groups=mesh['pa'=16,'row'=8] {'pa'}, dimensions={0} | all-to-all | bytes 8388608 | tf_op jit(solution)/shard_map/all_to_all | solution.py:130
  58.6 0.0 copy-done
  58.6 3.2 %doppler.1 = bf16[512,32,128]{2,1,0:T(8,128)(2,1)S(1)} custom-call(bf16[512,512]{1,0:T(8,128)(2,1)S(1)} %copy-done, bf16[16,2,32,16,128]{4,3,2,1,0:T(8,128)(2,1)S(1)} %all_to_all.10.samples_ref), custom_call_target="tpu_custom_call" | custom-call | tf_op jit(solution)/shard_map/doppler/pallas_call | solution.py:52
  61.8 0.0 copy-start.1
  61.8 60.2 %all_to_all.11 = bf16[128,2,2,32,128]{4,3,2,1,0:T(8,128)(2,1)S(1)} all-to-all(bf16[128,2,2,32,128]{4,3,2,1,0:T(8,128)(2,1)S(1)} %bitcast.7), channel_id=1, replica_groups=mesh['pa'=16,'row'=8] {'pa','row'}, dimensions={0} | all-to-all | bytes 8388608 | tf_op jit(solution)/shard_map/all_to_all | solution.py:133
  122.1 0.0 copy-done.1
  122.1 6.5 %covariances.1 = f32[2,2,128,128]{3,2,1,0:T(8,128)} custom-call(f32[1,256]{1,0:T(1,128)S(1)} %bitcast.9, bf16[16,8,2,2,32,128]{5,4,3,2,1,0:T(8,128)(2,1)S(1)} %bitcast.8), custom_call_target="tpu_custom_call" | custom-call | tf_op jit(solution)/shard_map/covariances/pallas_call | solution.py:111
Async XLA Ops:
  2.9 55.7 %copy-start = (bf16[512,512]{1,0:T(8,128)(2,1)S(1)}, bf16[512,512]{1,0:T(8,128)(2,1)}, u32[]{:S(2)}) copy-start(bf16[512,512]{1,0:T(8,128)(2,1)} %constant.2.clone.matrix_ref) | copy-start | bytes 1572868
  61.8 60.2 %copy-start.1 = (f32[256]{0:T(256)S(1)}, f32[256]{0:T(256)}, u32[]{:S(2)}) copy-start(f32[256]{0:T(256)} %param.4) | copy-start | bytes 3076

commit v4 on v3

--- a/solution.py
+++ b/solution.py
@@ -60,6 +60,37 @@
     )(matrix, samples)
 
 
+def repack_kernel(echoes_ref, out_ref, sems):
+    owners = out_ref.shape[0]
+    step = owners // sems.shape[1]
+    copies = [
+        pltpu.make_async_copy(
+            echoes_ref.at[part, pl.ds(k * step, step)],
+            out_ref.at[pl.ds(k * step, step), part],
+            sems.at[part, k],
+        )
+        for part in range(2)
+        for k in range(sems.shape[1])
+    ]
+    for copy in copies:
+        copy.start()
+    for copy in copies:
+        copy.wait()
+
+
+def repack(echoes):
+    shape = (echoes.shape[1], 2) + echoes.shape[2:]
+    return pl.pallas_call(
+        repack_kernel,
+        out_shape=jax.ShapeDtypeStruct(shape, echoes.dtype),
+        in_specs=[pl.BlockSpec(memory_space=pltpu.HBM)],
+        out_specs=pl.BlockSpec(memory_space=pltpu.VMEM),
+        scratch_shapes=[pltpu.SemaphoreType.DMA((2, 4))],
+        compiler_params=pltpu.CompilerParams(vmem_limit_bytes=8 << 20),
+        name="repack",
+    )(echoes)
+
+
 def covariance_kernel(total_gates, phase_ref, samples_ref, out_ref):
     pa_count, row_count, _, _, gates, n = samples_ref.shape
     b = pl.program_id(0)
@@ -96,7 +127,7 @@
         sums = [x if y is None else x + y for x, y in zip(sums, carried + [None])]
         carried = sums[1:]
         waiting.append(sums[0].astype(jnp.bfloat16))
-        if len(waiting) == reach:
+        if len(waiting) == 4 * reach:
             filtered = jnp.concatenate(waiting, axis=0)
             waiting = []
             gram = gram + lax.dot_general(
@@ -126,7 +157,8 @@
     devices = pa_count * row_count
     gates = gates_dev // pa_count
     bins = pulses // devices
-    blocks = echoes.reshape(2, pa_count, gates, pulses_dev, element_count).swapaxes(0, 1)
+    blocks = echoes.reshape(2, pa_count, gates, pulses_dev, element_count)
+    blocks = repack(pltpu.with_memory_space_constraint(blocks, pltpu.HBM))
     turned = lax.all_to_all(blocks, "pa", split_axis=0, concat_axis=0, tiled=True)
     spectrum = doppler(jnp.asarray(doppler_matrix(pulses)), turned)
     spectrum = spectrum.reshape(devices, bins, 2, gates, element_count)

time: 129 us -> 127 us (0.984)
  local copies, waits for them, and re-layouts: 2.92 us -> 0.01 us
  Pallas kernels: 9.65 us -> 11.3 us
    reshape x1 -> x0, local copies, waits for them, and re-layouts: 2.91 us -> none  [per_device(): echoes.reshape(2, pa_count, gates, pulses_dev, element_count).swapaxes(0, 1)]
    pallas_call x0 -> x1, Pallas kernels: none -> 2.21 us  [repack(): pl.pallas_call(repack_kernel, out_shape=jax.ShapeDtypeStruct(shape, echoe...]
where the time goes in v4:
time: 127 us
  blocking collectives  116 us (91%)
  Pallas kernels  11.3 us (9%)
    all_to_all x1, blocking collectives, per_device(): lax.all_to_all(spectrum, ('pa', 'row'), split_axis=0, concat_axis=0, tile...  60.2 us
    all_to_all x1, blocking collectives, per_device(): lax.all_to_all(blocks, 'pa', split_axis=0, concat_axis=0, tiled=True)  55.7 us
    pallas_call x1, Pallas kernels, covariances(): pl.pallas_call(functools.partial(covariance_kernel, total_gates), out_sha...  5.89 us
    pallas_call x1, Pallas kernels, doppler(): pl.pallas_call(doppler_kernel, out_shape=jax.ShapeDtypeStruct((rows, gate...  3.17 us

profile of v4, /device:TPU:0, one launch (start us, length us, event | category | flops | bytes accessed | tf_op | source)
XLA Modules:
  0.0 127.3 jit_solution(12976791206026669842)
XLA Ops:
  0.0 2.2 %repack.1 = bf16[16,2,32,16,128]{4,3,2,1,0:T(8,128)(2,1)S(1)} custom-call(bf16[2,16,32,16,128]{4,3,2,1,0:T(8,128)(2,1)} %bitcast.7), custom_call_target="tpu_custom_call" | custom-call | tf_op jit(solution)/shard_map/repack/pallas_call | solution.py:83
  2.2 0.0 copy-start
  2.2 55.7 %all_to_all.10.samples_ref = bf16[16,2,32,16,128]{4,3,2,1,0:T(8,128)(2,1)S(1)} all-to-all(bf16[16,2,32,16,128]{4,3,2,1,0:T(8,128)(2,1)S(1)} %repack.1), channel_id=1, replica_groups=mesh['pa'=16,'row'=8] {'pa'}, dimensions={0} | all-to-all | bytes 8388608 | tf_op jit(solution)/shard_map/all_to_all | solution.py:162
  57.9 0.0 copy-done
  57.9 3.2 %doppler.1 = bf16[512,32,128]{2,1,0:T(8,128)(2,1)S(1)} custom-call(bf16[512,512]{1,0:T(8,128)(2,1)S(1)} %copy-done, bf16[16,2,32,16,128]{4,3,2,1,0:T(8,128)(2,1)S(1)} %all_to_all.10.samples_ref), custom_call_target="tpu_custom_call" | custom-call | tf_op jit(solution)/shard_map/doppler/pallas_call | solution.py:52
  61.1 0.0 copy-start.1
  61.1 60.2 %all_to_all.11 = bf16[128,2,2,32,128]{4,3,2,1,0:T(8,128)(2,1)S(1)} all-to-all(bf16[128,2,2,32,128]{4,3,2,1,0:T(8,128)(2,1)S(1)} %bitcast.4), channel_id=1, replica_groups=mesh['pa'=16,'row'=8] {'pa','row'}, dimensions={0} | all-to-all | bytes 8388608 | tf_op jit(solution)/shard_map/all_to_all | solution.py:165
  121.4 0.0 copy-done.1
  121.4 5.9 %covariances.1 = f32[2,2,128,128]{3,2,1,0:T(8,128)} custom-call(f32[1,256]{1,0:T(1,128)S(1)} %bitcast.6, bf16[16,8,2,2,32,128]{5,4,3,2,1,0:T(8,128)(2,1)S(1)} %bitcast.5), custom_call_target="tpu_custom_call" | custom-call | tf_op jit(solution)/shard_map/covariances/pallas_call | solution.py:142
Async XLA Ops:
  2.2 55.7 %copy-start = (bf16[512,512]{1,0:T(8,128)(2,1)S(1)}, bf16[512,512]{1,0:T(8,128)(2,1)}, u32[]{:S(2)}) copy-start(bf16[512,512]{1,0:T(8,128)(2,1)} %constant.2.clone.matrix_ref) | copy-start | bytes 1572868
  61.1 60.2 %copy-start.1 = (f32[256]{0:T(256)S(1)}, f32[256]{0:T(256)}, u32[]{:S(2)}) copy-start(f32[256]{0:T(256)} %param.4) | copy-start | bytes 3076

commit v5 on v4

--- a/solution.py
+++ b/solution.py
@@ -92,8 +92,7 @@
 
 
 def covariance_kernel(total_gates, phase_ref, samples_ref, out_ref):
-    pa_count, row_count, _, _, gates, n = samples_ref.shape
-    b = pl.program_id(0)
+    pa_count, row_count, bins, _, gates, n = samples_ref.shape
     taps = phase_ref.shape[1]
     reach = 2
     tile = taps // reach
@@ -111,30 +110,32 @@
     parts = [slice(k * tile, (k + 1) * tile) for k in range(reach + 1)]
     bands = [jnp.concatenate([real_band[:, k], imag_band[:, k]], axis=1) for k in parts]
     bands = jnp.concatenate(bands, axis=0)
-    gram = jnp.zeros((2 * n, 2 * n), jnp.float32)
     carried = [None] * reach
-    waiting = []
+    filtered = []
     for t in reversed(range(row_count * tiles_row)):
         row, first = t // tiles_row, t % tiles_row * owners
-        real, imag = (
-            samples_ref[first : first + owners, row, b, part].reshape(tile, n) for part in range(2)
-        )
-        upper = jnp.concatenate([real, imag], axis=1)
-        lower = jnp.concatenate([-imag, real], axis=1)
-        both = jnp.concatenate([upper, lower], axis=0)
-        product = jnp.dot(bands, both, preferred_element_type=jnp.float32)
+        columns = []
+        for b in range(bins):
+            real, imag = (
+                samples_ref[first : first + owners, row, b, part].reshape(tile, n) for part in range(2)
+            )
+            upper = jnp.concatenate([real, imag], axis=1)
+            lower = jnp.concatenate([-imag, real], axis=1)
+            columns.append(jnp.concatenate([upper, lower], axis=0))
+        columns = jnp.concatenate(columns, axis=1)
+        product = jnp.dot(bands, columns, preferred_element_type=jnp.float32)
         sums = [product[k] for k in parts]
         sums = [x if y is None else x + y for x, y in zip(sums, carried + [None])]
         carried = sums[1:]
-        waiting.append(sums[0].astype(jnp.bfloat16))
-        if len(waiting) == 4 * reach:
-            filtered = jnp.concatenate(waiting, axis=0)
-            waiting = []
-            gram = gram + lax.dot_general(
-                filtered, filtered, (((0,), (0,)), ((), ())), preferred_element_type=jnp.float32
-            )
-    out_ref[0, 0] = (gram[:n, :n] + gram[n:, n:]) / total_gates
-    out_ref[0, 1] = (gram[n:, :n] - gram[:n, n:]) / total_gates
+        filtered.append(sums[0].astype(jnp.bfloat16))
+    filtered = jnp.concatenate(filtered, axis=0)
+    for b in range(bins):
+        one = filtered[:, b * 2 * n : (b + 1) * 2 * n]
+        gram = lax.dot_general(
+            one, one, (((0,), (0,)), ((), ())), preferred_element_type=jnp.float32
+        )
+        out_ref[b, 0] = (gram[:n, :n] + gram[n:, n:]) / total_gates
+        out_ref[b, 1] = (gram[n:, :n] - gram[:n, n:]) / total_gates
 
 
 def covariances(phase, samples, total_gates):
@@ -142,10 +143,9 @@
     return pl.pallas_call(
         functools.partial(covariance_kernel, total_gates),
         out_shape=jax.ShapeDtypeStruct((bins, 2, element_count, element_count), jnp.float32),
-        grid=(bins,),
         in_specs=[pl.BlockSpec(memory_space=pltpu.VMEM)] * 2,
-        out_specs=pl.BlockSpec((1, 2, element_count, element_count), lambda b: (b, 0, 0, 0)),
-        compiler_params=pltpu.CompilerParams(vmem_limit_bytes=20 << 20),
+        out_specs=pl.BlockSpec(memory_space=pltpu.VMEM),
+        compiler_params=pltpu.CompilerParams(vmem_limit_bytes=24 << 20),
         name="covariances",
     )(phase, samples)
 

time: 127 us -> 127 us (level)
  no operation moved by 1% of the time
where the time goes in v5:
time: 127 us
  blocking collectives  116 us (91%)
  Pallas kernels  10.7 us (8%)
    all_to_all x1, blocking collectives, per_device(): lax.all_to_all(spectrum, ('pa', 'row'), split_axis=0, concat_axis=0, tile...  60.2 us
    all_to_all x1, blocking collectives, per_device(): lax.all_to_all(blocks, 'pa', split_axis=0, concat_axis=0, tiled=True)  55.7 us
    pallas_call x1, Pallas kernels, covariances(): pl.pallas_call(functools.partial(covariance_kernel, total_gates), out_sha...  5.34 us
    pallas_call x1, Pallas kernels, doppler(): pl.pallas_call(doppler_kernel, out_shape=jax.ShapeDtypeStruct((rows, gate...  3.17 us

profile of v5, /device:TPU:0, one launch (start us, length us, event | category | flops | bytes accessed | tf_op | source)
XLA Modules:
  0.0 126.7 jit_solution(7098503947638235495)
XLA Ops:
  0.0 2.2 %repack.1 = bf16[16,2,32,16,128]{4,3,2,1,0:T(8,128)(2,1)S(1)} custom-call(bf16[2,16,32,16,128]{4,3,2,1,0:T(8,128)(2,1)} %bitcast.7), custom_call_target="tpu_custom_call" | custom-call | tf_op jit(solution)/shard_map/repack/pallas_call | solution.py:83
  2.2 0.0 copy-start
  2.2 55.7 %all_to_all.10.samples_ref = bf16[16,2,32,16,128]{4,3,2,1,0:T(8,128)(2,1)S(1)} all-to-all(bf16[16,2,32,16,128]{4,3,2,1,0:T(8,128)(2,1)S(1)} %repack.1), channel_id=1, replica_groups=mesh['pa'=16,'row'=8] {'pa'}, dimensions={0} | all-to-all | bytes 8388608 | tf_op jit(solution)/shard_map/all_to_all | solution.py:162
  57.9 0.0 copy-done
  57.9 3.2 %doppler.1 = bf16[512,32,128]{2,1,0:T(8,128)(2,1)S(1)} custom-call(bf16[512,512]{1,0:T(8,128)(2,1)S(1)} %copy-done, bf16[16,2,32,16,128]{4,3,2,1,0:T(8,128)(2,1)S(1)} %all_to_all.10.samples_ref), custom_call_target="tpu_custom_call" | custom-call | tf_op jit(solution)/shard_map/doppler/pallas_call | solution.py:52
  61.1 0.0 copy-start.1
  61.1 60.2 %all_to_all.11 = bf16[128,2,2,32,128]{4,3,2,1,0:T(8,128)(2,1)S(1)} all-to-all(bf16[128,2,2,32,128]{4,3,2,1,0:T(8,128)(2,1)S(1)} %bitcast.4), channel_id=1, replica_groups=mesh['pa'=16,'row'=8] {'pa','row'}, dimensions={0} | all-to-all | bytes 8388608 | tf_op jit(solution)/shard_map/all_to_all | solution.py:165
  121.4 0.0 copy-done.1
  121.4 5.3 %covariances.1 = f32[2,2,128,128]{3,2,1,0:T(8,128)} custom-call(f32[1,256]{1,0:T(1,128)S(1)} %bitcast.6, bf16[16,8,2,2,32,128]{5,4,3,2,1,0:T(8,128)(2,1)S(1)} %bitcast.5), custom_call_target="tpu_custom_call" | custom-call | tf_op jit(solution)/shard_map/covariances/pallas_call | solution.py:143
Async XLA Ops:
  2.2 55.7 %copy-start = (bf16[512,512]{1,0:T(8,128)(2,1)S(1)}, bf16[512,512]{1,0:T(8,128)(2,1)}, u32[]{:S(2)}) copy-start(bf16[512,512]{1,0:T(8,128)(2,1)} %constant.2.clone.matrix_ref) | copy-start | bytes 1572868
  61.1 60.2 %copy-start.1 = (f32[256]{0:T(256)S(1)}, f32[256]{0:T(256)}, u32[]{:S(2)}) copy-start(f32[256]{0:T(256)} %param.4) | copy-start | bytes 3076

commit v6 on v5

--- a/solution.py
+++ b/solution.py
@@ -10,54 +10,71 @@
 from jax.sharding import PartitionSpec as P
 
 
-def doppler_matrix(pulses):
-    indices = np.arange(pulses)
-    products = indices[:, None] * indices[None, :] % pulses
+def doppler_rows(pulses):
+    half = pulses // 2
+    products = np.arange(half + 1)[:, None] * np.arange(pulses)[None, :] % pulses
     angles = (np.float32(2.0 * math.pi / pulses) * products.astype(np.float32)).astype(np.float64)
     scaling = 1.0 / math.sqrt(pulses)
-    real_part = (np.cos(angles) * scaling).astype(np.float32)
-    imag_part = (-np.sin(angles) * scaling).astype(np.float32)
-    upper_half = np.stack([real_part, -imag_part], axis=1)
-    lower_half = np.stack([imag_part, real_part], axis=1)
-    matrix = np.stack([upper_half, lower_half], axis=1)
-    return matrix.reshape(2 * pulses, 2 * pulses).astype(jnp.bfloat16)
+    rows = np.concatenate([np.cos(angles), np.sin(angles[1:half])], axis=0) * scaling
+    return rows.astype(np.float32).astype(jnp.bfloat16)
 
 
-def doppler_kernel(matrix_ref, samples_ref, out_ref, scratch):
-    rows = matrix_ref.shape[0]
-    gates, element_count = out_ref.shape[1:]
-    slots, group = scratch.shape[:2]
+def doppler_kernel(rows_ref, samples_ref, out_ref, scratch):
+    pulses = rows_ref.shape[0]
+    half = pulses // 2
+    gates, n = out_ref.shape[1:]
+    slots, _, group = scratch.shape[:3]
+    step = 8
+    top = lax.broadcasted_iota(jnp.int32, (step, n), 0) == 0
 
-    def columns(gate):
-        parts = [samples_ref[:, part, gate].reshape(-1, element_count) for part in range(2)]
-        return jnp.concatenate(parts, axis=0)
+    def turn(first, slot, low, high):
+        for kind in range(4):
+            for row in range(low, high, step):
+                block = jnp.transpose(scratch[slot, kind, :, row : row + step, :], (1, 0, 2))
+                block = block.astype(jnp.bfloat16)
+                for j in range(step):
+                    b = row + j
+                    if kind >= 2:
+                        b = pulses - b if b else half
+                    out_ref[2 * b + kind % 2, first : first + group] = block[j]
 
-    step = 32
     for first in range(0, gates, group):
         slot = first // group % slots
-        for k in range(0, group, 2):
-            both = jnp.concatenate([columns(first + k), columns(first + k + 1)], axis=1)
-            product = jnp.dot(matrix_ref[...], both, preferred_element_type=jnp.float32)
-            scratch[slot, k] = product[:, :element_count]
-            scratch[slot, k + 1] = product[:, element_count:]
-        for row in range(0, rows, step):
-            block = jnp.transpose(scratch[slot, :, row : row + step, :], (1, 0, 2))
-            out_ref[row : row + step, first : first + group] = block.astype(jnp.bfloat16)
+        for k in range(group):
+            parts = [samples_ref[:, part, first + k].reshape(-1, n) for part in range(2)]
+            product = jnp.dot(
+                rows_ref[...], jnp.concatenate(parts, axis=1), preferred_element_type=jnp.float32
+            )
+            cos_real, cos_imag = product[:half, :n], product[:half, n:]
+            sin_real, sin_imag = product[half:, :n], product[half:, n:]
+            values = (
+                cos_real + sin_imag,
+                cos_imag - sin_real,
+                cos_real - sin_imag,
+                cos_imag + sin_real,
+            )
+            tops = (cos_real, cos_imag, sin_real, sin_imag)
+            for kind in range(4):
+                scratch[slot, kind, k] = values[kind]
+                scratch[slot, kind, k, :step] = jnp.where(top, tops[kind][:step], values[kind][:step])
+            if first:
+                turn(first - group, 1 - slot, half * k // group, half * (k + 1) // group)
+    turn(gates - group, (gates // group - 1) % slots, 0, half)
 
 
-def doppler(matrix, samples):
-    gates, _, element_count = samples.shape[2:]
-    rows = matrix.shape[0]
+def doppler(rows, samples):
+    gates, _, n = samples.shape[2:]
+    pulses = rows.shape[0]
     group = math.gcd(16, gates)
     return pl.pallas_call(
         doppler_kernel,
-        out_shape=jax.ShapeDtypeStruct((rows, gates, element_count), jnp.bfloat16),
+        out_shape=jax.ShapeDtypeStruct((2 * pulses, gates, n), jnp.bfloat16),
         in_specs=[pl.BlockSpec(memory_space=pltpu.VMEM)] * 2,
         out_specs=pl.BlockSpec(memory_space=pltpu.VMEM),
-        scratch_shapes=[pltpu.VMEM((2, group, rows, element_count), jnp.float32)],
+        scratch_shapes=[pltpu.VMEM((2, 4, group, pulses // 2, n), jnp.float32)],
         compiler_params=pltpu.CompilerParams(vmem_limit_bytes=24 << 20),
         name="doppler",
-    )(matrix, samples)
+    )(rows, samples)
 
 
 def repack_kernel(echoes_ref, out_ref, sems):
@@ -160,7 +177,7 @@
     blocks = echoes.reshape(2, pa_count, gates, pulses_dev, element_count)
     blocks = repack(pltpu.with_memory_space_constraint(blocks, pltpu.HBM))
     turned = lax.all_to_all(blocks, "pa", split_axis=0, concat_axis=0, tiled=True)
-    spectrum = doppler(jnp.asarray(doppler_matrix(pulses)), turned)
+    spectrum = doppler(jnp.asarray(doppler_rows(pulses)), turned)
     spectrum = spectrum.reshape(devices, bins, 2, gates, element_count)
     owned = lax.all_to_all(spectrum, ("pa", "row"), split_axis=0, concat_axis=0, tiled=True)
     owned = owned.reshape(pa_count, row_count, bins, 2, gates, element_count)

time: 127 us -> 126 us (level)
  no operation moved by 1% of the time
where the time goes in v6:
time: 126 us
  blocking collectives  116 us (92%)
  Pallas kernels  10.2 us (8%)
    all_to_all x1, blocking collectives, per_device(): lax.all_to_all(spectrum, ('pa', 'row'), split_axis=0, concat_axis=0, tile...  60.2 us
    all_to_all x1, blocking collectives, per_device(): lax.all_to_all(blocks, 'pa', split_axis=0, concat_axis=0, tiled=True)  55.7 us
    pallas_call x1, Pallas kernels, covariances(): pl.pallas_call(functools.partial(covariance_kernel, total_gates), out_sha...  5.34 us
    pallas_call x1, Pallas kernels, doppler(): pl.pallas_call(doppler_kernel, out_shape=jax.ShapeDtypeStruct((2 * pulses...  2.68 us

profile of v6, /device:TPU:0, one launch (start us, length us, event | category | flops | bytes accessed | tf_op | source)
XLA Modules:
  0.0 126.2 jit_solution(7582295124325869511)
XLA Ops:
  0.0 2.2 %repack.1 = bf16[16,2,32,16,128]{4,3,2,1,0:T(8,128)(2,1)S(1)} custom-call(bf16[2,16,32,16,128]{4,3,2,1,0:T(8,128)(2,1)} %bitcast.7), custom_call_target="tpu_custom_call" | custom-call | tf_op jit(solution)/shard_map/repack/pallas_call | solution.py:100
  2.2 0.0 copy-start
  2.2 55.7 %all_to_all.10.samples_ref = bf16[16,2,32,16,128]{4,3,2,1,0:T(8,128)(2,1)S(1)} all-to-all(bf16[16,2,32,16,128]{4,3,2,1,0:T(8,128)(2,1)S(1)} %repack.1), channel_id=1, replica_groups=mesh['pa'=16,'row'=8] {'pa'}, dimensions={0} | all-to-all | bytes 8388608 | tf_op jit(solution)/shard_map/all_to_all | solution.py:179
  57.9 0.0 copy-done
  57.9 2.7 %doppler.1 = bf16[512,32,128]{2,1,0:T(8,128)(2,1)S(1)} custom-call(bf16[256,256]{1,0:T(8,128)(2,1)S(1)} %copy-done, bf16[16,2,32,16,128]{4,3,2,1,0:T(8,128)(2,1)S(1)} %all_to_all.10.samples_ref), custom_call_target="tpu_custom_call" | custom-call | tf_op jit(solution)/shard_map/doppler/pallas_call | solution.py:69
  60.6 0.0 copy-start.1
  60.6 60.2 %all_to_all.11 = bf16[128,2,2,32,128]{4,3,2,1,0:T(8,128)(2,1)S(1)} all-to-all(bf16[128,2,2,32,128]{4,3,2,1,0:T(8,128)(2,1)S(1)} %bitcast.4), channel_id=1, replica_groups=mesh['pa'=16,'row'=8] {'pa','row'}, dimensions={0} | all-to-all | bytes 8388608 | tf_op jit(solution)/shard_map/all_to_all | solution.py:182
  120.9 0.0 copy-done.1
  120.9 5.3 %covariances.1 = f32[2,2,128,128]{3,2,1,0:T(8,128)} custom-call(f32[1,256]{1,0:T(1,128)S(1)} %bitcast.6, bf16[16,8,2,2,32,128]{5,4,3,2,1,0:T(8,128)(2,1)S(1)} %bitcast.5), custom_call_target="tpu_custom_call" | custom-call | tf_op jit(solution)/shard_map/covariances/pallas_call | solution.py:160
Async XLA Ops:
  2.2 55.7 %copy-start = (bf16[256,256]{1,0:T(8,128)(2,1)S(1)}, bf16[256,256]{1,0:T(8,128)(2,1)}, u32[]{:S(2)}) copy-start(bf16[256,256]{1,0:T(8,128)(2,1)} %constant.2.clone.rows_ref) | copy-start | bytes 393220
  60.6 60.3 %copy-start.1 = (f32[256]{0:T(256)S(1)}, f32[256]{0:T(256)}, u32[]{:S(2)}) copy-start(f32[256]{0:T(256)} %param.4) | copy-start | bytes 3076

commit v7 on v6

--- a/solution.py
+++ b/solution.py
@@ -7,7 +7,13 @@
 from jax import lax
 from jax.experimental import pallas as pl
 from jax.experimental.pallas import tpu as pltpu
+from jax.sharding import Mesh
 from jax.sharding import PartitionSpec as P
+
+
+PA = ("xl", "y", "core")
+ROW = ("z", "xh")
+EXCHANGE = ("z", "y", "xh", "xl", "core")
 
 
 def doppler_rows(pulses):
@@ -19,7 +25,7 @@
     return rows.astype(np.float32).astype(jnp.bfloat16)
 
 
-def doppler_kernel(rows_ref, samples_ref, out_ref, scratch):
+def doppler_kernel(places, rows_ref, samples_ref, out_ref, scratch):
     pulses = rows_ref.shape[0]
     half = pulses // 2
     gates, n = out_ref.shape[1:]
@@ -36,7 +42,7 @@
                     b = row + j
                     if kind >= 2:
                         b = pulses - b if b else half
-                    out_ref[2 * b + kind % 2, first : first + group] = block[j]
+                    out_ref[2 * places[b] + kind % 2, first : first + group] = block[j]
 
     for first in range(0, gates, group):
         slot = first // group % slots
@@ -62,12 +68,12 @@
     turn(gates - group, (gates // group - 1) % slots, 0, half)
 
 
-def doppler(rows, samples):
+def doppler(rows, samples, places):
     gates, _, n = samples.shape[2:]
     pulses = rows.shape[0]
     group = math.gcd(16, gates)
     return pl.pallas_call(
-        doppler_kernel,
+        functools.partial(doppler_kernel, places),
         out_shape=jax.ShapeDtypeStruct((2 * pulses, gates, n), jnp.bfloat16),
         in_specs=[pl.BlockSpec(memory_space=pltpu.VMEM)] * 2,
         out_specs=pl.BlockSpec(memory_space=pltpu.VMEM),
@@ -109,7 +115,10 @@
 
 
 def covariance_kernel(total_gates, phase_ref, samples_ref, out_ref):
-    pa_count, row_count, bins, _, gates, n = samples_ref.shape
+    sizes = dict(zip(EXCHANGE, samples_ref.shape))
+    bins, _, gates, n = samples_ref.shape[5:]
+    pa_count = sizes["xl"] * sizes["y"] * sizes["core"]
+    row_count = sizes["z"] * sizes["xh"]
     taps = phase_ref.shape[1]
     reach = 2
     tile = taps // reach
@@ -129,12 +138,29 @@
     bands = jnp.concatenate(bands, axis=0)
     carried = [None] * reach
     filtered = []
-    for t in reversed(range(row_count * tiles_row)):
+    ready = []
+    tiles = row_count * tiles_row
+    grams = [jnp.zeros((2 * n, 2 * n), jnp.float32)] * bins
+
+    def added(rows):
+        columns = [rows[:, b * 2 * n : (b + 1) * 2 * n] for b in range(bins)]
+        return [
+            gram
+            + lax.dot_general(
+                one, one, (((0,), (0,)), ((), ())), preferred_element_type=jnp.float32
+            )
+            for gram, one in zip(grams, columns)
+        ]
+
+    for t in reversed(range(tiles)):
         row, first = t // tiles_row, t % tiles_row * owners
+        z, xh = divmod(row, sizes["xh"])
+        xl, y = divmod(first // sizes["core"], sizes["y"])
+        ys = slice(y, y + owners // sizes["core"])
         columns = []
         for b in range(bins):
             real, imag = (
-                samples_ref[first : first + owners, row, b, part].reshape(tile, n) for part in range(2)
+                samples_ref[z, ys, xh, xl, :, b, part].reshape(tile, n) for part in range(2)
             )
             upper = jnp.concatenate([real, imag], axis=1)
             lower = jnp.concatenate([-imag, real], axis=1)
@@ -145,18 +171,18 @@
         sums = [x if y is None else x + y for x, y in zip(sums, carried + [None])]
         carried = sums[1:]
         filtered.append(sums[0].astype(jnp.bfloat16))
-    filtered = jnp.concatenate(filtered, axis=0)
-    for b in range(bins):
-        one = filtered[:, b * 2 * n : (b + 1) * 2 * n]
-        gram = lax.dot_general(
-            one, one, (((0,), (0,)), ((), ())), preferred_element_type=jnp.float32
-        )
+        if len(filtered) == tiles // 2:
+            if ready:
+                grams = added(jnp.concatenate(ready, axis=0))
+            ready, filtered = filtered, []
+    grams = added(jnp.concatenate(ready, axis=0))
+    for b, gram in enumerate(grams):
         out_ref[b, 0] = (gram[:n, :n] + gram[n:, n:]) / total_gates
         out_ref[b, 1] = (gram[n:, :n] - gram[:n, n:]) / total_gates
 
 
 def covariances(phase, samples, total_gates):
-    bins, element_count = samples.shape[2], samples.shape[-1]
+    bins, element_count = samples.shape[5], samples.shape[-1]
     return pl.pallas_call(
         functools.partial(covariance_kernel, total_gates),
         out_shape=jax.ShapeDtypeStruct((bins, 2, element_count, element_count), jnp.float32),
@@ -169,27 +195,33 @@
 
 def per_device(echoes, chirp_phase):
     gates_dev, pulses_dev, element_count = echoes.shape[1:]
-    pa_count, row_count = lax.axis_size("pa"), lax.axis_size("row")
+    sizes = {axis: lax.axis_size(axis) for axis in PA + ROW}
+    pa_count, row_count = math.prod(sizes[a] for a in PA), math.prod(sizes[a] for a in ROW)
     pulses, total_gates = pulses_dev * pa_count, gates_dev * row_count
     devices = pa_count * row_count
     gates = gates_dev // pa_count
     bins = pulses // devices
+    owners = np.arange(devices).reshape([sizes[a] for a in PA + ROW])
+    order = owners.transpose([(PA + ROW).index(a) for a in EXCHANGE]).reshape(-1)
+    position = np.argsort(order)
+    places = [int(position[b // bins]) * bins + b % bins for b in range(pulses)]
     blocks = echoes.reshape(2, pa_count, gates, pulses_dev, element_count)
     blocks = repack(pltpu.with_memory_space_constraint(blocks, pltpu.HBM))
-    turned = lax.all_to_all(blocks, "pa", split_axis=0, concat_axis=0, tiled=True)
-    spectrum = doppler(jnp.asarray(doppler_rows(pulses)), turned)
+    turned = lax.all_to_all(blocks, PA, split_axis=0, concat_axis=0, tiled=True)
+    spectrum = doppler(jnp.asarray(doppler_rows(pulses)), turned, places)
     spectrum = spectrum.reshape(devices, bins, 2, gates, element_count)
-    owned = lax.all_to_all(spectrum, ("pa", "row"), split_axis=0, concat_axis=0, tiled=True)
-    owned = owned.reshape(pa_count, row_count, bins, 2, gates, element_count)
+    owned = lax.all_to_all(spectrum, EXCHANGE, split_axis=0, concat_axis=0, tiled=True)
+    owned = owned.reshape([sizes[a] for a in EXCHANGE] + [bins, 2, gates, element_count])
     return covariances(chirp_phase[None], owned, total_gates)
 
 
 def solution(mesh):
-    placed = (P(None, "row", "pa", None), P())
+    pa_count, row_count = mesh.shape["pa"], mesh.shape["row"]
+    devices = mesh.devices.reshape(2, pa_count // 4, 2, row_count // 2, 2)
     return jax.shard_map(
         per_device,
-        mesh=mesh,
-        in_specs=placed,
-        out_specs=P(("pa", "row"), None, None, None),
+        mesh=Mesh(devices, PA + ROW),
+        in_specs=(P(None, ROW, PA, None), P()),
+        out_specs=P(PA + ROW, None, None, None),
         check_vma=False,
     )

time: 126 us -> 128 us (1.016)
  no operation moved by 1% of the time
where the time goes in v7:
time: 128 us; the launch traced here: 127 us
  blocking collectives  117 us (91%)
  Pallas kernels  10.2 us (8%)
    all_to_all x1, blocking collectives, per_device(): lax.all_to_all(spectrum, EXCHANGE, split_axis=0, concat_axis=0, tiled=True)  61.1 us
    all_to_all x1, blocking collectives, per_device(): turned = lax.all_to_all(blocks, PA, split_axis=0, concat_axis=0, tiled=True)  55.7 us
    pallas_call x1, Pallas kernels, covariances(): pl.pallas_call(functools.partial(covariance_kernel, total_gates), out_sha...  5.33 us
    pallas_call x1, Pallas kernels, doppler(): pl.pallas_call(functools.partial(doppler_kernel, places), out_shape=jax.S...  2.68 us

profile of v7, /device:TPU:0, one launch (start us, length us, event | category | flops | bytes accessed | tf_op | source)
XLA Modules:
  0.0 127.1 jit_solution(8563789203621540378)
XLA Ops:
  0.0 2.2 %repack.1 = bf16[16,2,32,16,128]{4,3,2,1,0:T(8,128)(2,1)S(1)} custom-call(bf16[2,16,32,16,128]{4,3,2,1,0:T(8,128)(2,1)} %bitcast.7), custom_call_target="tpu_custom_call" | custom-call | tf_op jit(solution)/shard_map/repack/pallas_call | solution.py:106
  2.2 0.0 copy-start
  2.2 55.7 %all_to_all.10.samples_ref = bf16[16,2,32,16,128]{4,3,2,1,0:T(8,128)(2,1)S(1)} all-to-all(bf16[16,2,32,16,128]{4,3,2,1,0:T(8,128)(2,1)S(1)} %repack.1), channel_id=1, replica_groups=mesh['xl'=2,'y'=4,'core'=2,'z'=4,'xh'=2] {'xl','y','core'}, dimensions={0} | all-to-all | bytes 8388608 | tf_op jit(solution)/shard_map/all_to_all | solution.py:210
  57.9 0.0 copy-done
  57.9 2.7 %doppler.1 = bf16[512,32,128]{2,1,0:T(8,128)(2,1)S(1)} custom-call(bf16[256,256]{1,0:T(8,128)(2,1)S(1)} %copy-done, bf16[16,2,32,16,128]{4,3,2,1,0:T(8,128)(2,1)S(1)} %all_to_all.10.samples_ref), custom_call_target="tpu_custom_call" | custom-call | tf_op jit(solution)/shard_map/doppler/pallas_call | solution.py:75
  60.6 0.0 copy-start.1
  60.6 61.1 %all_to_all.11 = bf16[128,2,2,32,128]{4,3,2,1,0:T(8,128)(2,1)S(1)} all-to-all(bf16[128,2,2,32,128]{4,3,2,1,0:T(8,128)(2,1)S(1)} %bitcast.4), channel_id=1, replica_groups=mesh['xl'=2,'y'=4,'core'=2,'z'=4,'xh'=2] {'z','y','xh','xl','core'}, dimensions={0} | all-to-all | bytes 8388608 | tf_op jit(solution)/shard_map/all_to_all | solution.py:213
  121.8 0.0 copy-done.1
  121.8 5.3 %covariances.1 = f32[2,2,128,128]{3,2,1,0:T(8,128)} custom-call(f32[1,256]{1,0:T(1,128)S(1)} %bitcast.6, bf16[4,4,2,2,2,2,2,32,128]{8,7,6,5,4,3,2,1,0:T(8,128)(2,1)S(1)} %bitcast.5), custom_call_target="tpu_custom_call" | custom-call | tf_op jit(solution)/shard_map/covariances/pallas_call | solution.py:186
Async XLA Ops:
  2.2 55.7 %copy-start = (bf16[256,256]{1,0:T(8,128)(2,1)S(1)}, bf16[256,256]{1,0:T(8,128)(2,1)}, u32[]{:S(2)}) copy-start(bf16[256,256]{1,0:T(8,128)(2,1)} %constant.2.clone.rows_ref) | copy-start | bytes 393220
  60.6 61.1 %copy-start.1 = (f32[256]{0:T(256)S(1)}, f32[256]{0:T(256)}, u32[]{:S(2)}) copy-start(f32[256]{0:T(256)} %param.4) | copy-start | bytes 3076

commit v8 on v6

--- a/solution.py
+++ b/solution.py
@@ -77,7 +77,27 @@
     )(rows, samples)
 
 
-def repack_kernel(echoes_ref, out_ref, sems):
+REACH = 2
+
+
+def band_rows(phase):
+    taps = phase.shape[1]
+    tile = taps // REACH
+    scaling = 1.0 / math.sqrt(taps)
+
+    def band(values):
+        values = (values * scaling).astype(jnp.bfloat16).astype(jnp.float32)
+        values = jnp.concatenate([values, jnp.zeros((1, tile), jnp.float32)], axis=1)
+        values = jnp.broadcast_to(values, (tile, taps + tile))
+        return pltpu.roll(values, 0, 1, stride=1, stride_axis=0).astype(jnp.bfloat16)
+
+    real_band, imag_band = band(jnp.cos(phase)), band(-jnp.sin(phase))
+    parts = [slice(k * tile, (k + 1) * tile) for k in range(REACH + 1)]
+    bands = [jnp.concatenate([real_band[:, k], imag_band[:, k]], axis=1) for k in parts]
+    return jnp.concatenate(bands, axis=0)
+
+
+def repack_kernel(phase_ref, echoes_ref, out_ref, bands_ref, phase, phase_sem, sems):
     owners = out_ref.shape[0]
     step = owners // sems.shape[1]
     copies = [
@@ -89,45 +109,45 @@
         for part in range(2)
         for k in range(sems.shape[1])
     ]
+    fetch = pltpu.make_async_copy(phase_ref, phase, phase_sem)
+    fetch.start()
     for copy in copies:
         copy.start()
+    fetch.wait()
+    bands_ref[...] = band_rows(phase[...])
     for copy in copies:
         copy.wait()
 
 
-def repack(echoes):
+def repack(phase, echoes):
     shape = (echoes.shape[1], 2) + echoes.shape[2:]
+    tile = phase.shape[1] // REACH
     return pl.pallas_call(
         repack_kernel,
-        out_shape=jax.ShapeDtypeStruct(shape, echoes.dtype),
-        in_specs=[pl.BlockSpec(memory_space=pltpu.HBM)],
-        out_specs=pl.BlockSpec(memory_space=pltpu.VMEM),
-        scratch_shapes=[pltpu.SemaphoreType.DMA((2, 4))],
+        out_shape=[
+            jax.ShapeDtypeStruct(shape, echoes.dtype),
+            jax.ShapeDtypeStruct(((REACH + 1) * tile, 2 * tile), jnp.bfloat16),
+        ],
+        in_specs=[pl.BlockSpec(memory_space=pltpu.HBM)] * 2,
+        out_specs=[pl.BlockSpec(memory_space=pltpu.VMEM)] * 2,
+        scratch_shapes=[
+            pltpu.VMEM(phase.shape, phase.dtype),
+            pltpu.SemaphoreType.DMA,
+            pltpu.SemaphoreType.DMA((2, 4)),
+        ],
         compiler_params=pltpu.CompilerParams(vmem_limit_bytes=8 << 20),
         name="repack",
-    )(echoes)
-
-
-def covariance_kernel(total_gates, phase_ref, samples_ref, out_ref):
+    )(phase, echoes)
+
+
+def covariance_kernel(total_gates, bands_ref, samples_ref, out_ref):
     pa_count, row_count, bins, _, gates, n = samples_ref.shape
-    taps = phase_ref.shape[1]
-    reach = 2
-    tile = taps // reach
+    bands = bands_ref[...]
+    tile = bands.shape[1] // 2
     owners = tile // gates
     tiles_row = pa_count // owners
-    scaling = 1.0 / math.sqrt(taps)
-
-    def band(values):
-        values = (values * scaling).astype(jnp.bfloat16).astype(jnp.float32)
-        values = jnp.concatenate([values, jnp.zeros((1, tile), jnp.float32)], axis=1)
-        values = jnp.broadcast_to(values, (tile, taps + tile))
-        return pltpu.roll(values, 0, 1, stride=1, stride_axis=0).astype(jnp.bfloat16)
-
-    real_band, imag_band = band(jnp.cos(phase_ref[...])), band(-jnp.sin(phase_ref[...]))
-    parts = [slice(k * tile, (k + 1) * tile) for k in range(reach + 1)]
-    bands = [jnp.concatenate([real_band[:, k], imag_band[:, k]], axis=1) for k in parts]
-    bands = jnp.concatenate(bands, axis=0)
-    carried = [None] * reach
+    parts = [slice(k * tile, (k + 1) * tile) for k in range(REACH + 1)]
+    carried = [None] * REACH
     filtered = []
     for t in reversed(range(row_count * tiles_row)):
         row, first = t // tiles_row, t % tiles_row * owners
@@ -155,7 +175,7 @@
         out_ref[b, 1] = (gram[n:, :n] - gram[:n, n:]) / total_gates
 
 
-def covariances(phase, samples, total_gates):
+def covariances(bands, samples, total_gates):
     bins, element_count = samples.shape[2], samples.shape[-1]
     return pl.pallas_call(
         functools.partial(covariance_kernel, total_gates),
@@ -164,7 +184,7 @@
         out_specs=pl.BlockSpec(memory_space=pltpu.VMEM),
         compiler_params=pltpu.CompilerParams(vmem_limit_bytes=24 << 20),
         name="covariances",
-    )(phase, samples)
+    )(bands, samples)
 
 
 def per_device(echoes, chirp_phase):
@@ -175,13 +195,15 @@
     gates = gates_dev // pa_count
     bins = pulses // devices
     blocks = echoes.reshape(2, pa_count, gates, pulses_dev, element_count)
-    blocks = repack(pltpu.with_memory_space_constraint(blocks, pltpu.HBM))
+    blocks = pltpu.with_memory_space_constraint(blocks, pltpu.HBM)
+    phase = pltpu.with_memory_space_constraint(chirp_phase[None], pltpu.HBM)
+    blocks, bands = repack(phase, blocks)
     turned = lax.all_to_all(blocks, "pa", split_axis=0, concat_axis=0, tiled=True)
     spectrum = doppler(jnp.asarray(doppler_rows(pulses)), turned)
     spectrum = spectrum.reshape(devices, bins, 2, gates, element_count)
     owned = lax.all_to_all(spectrum, ("pa", "row"), split_axis=0, concat_axis=0, tiled=True)
     owned = owned.reshape(pa_count, row_count, bins, 2, gates, element_count)
-    return covariances(chirp_phase[None], owned, total_gates)
+    return covariances(bands, owned, total_gates)
 
 
 def solution(mesh):

time: 126 us -> 126 us (level)
  no operation moved by 1% of the time
where the time goes in v8:
time: 126 us
  blocking collectives  116 us (92%)
  Pallas kernels  10.1 us (8%)
    all_to_all x1, blocking collectives, per_device(): lax.all_to_all(spectrum, ('pa', 'row'), split_axis=0, concat_axis=0, tile...  60.2 us
    all_to_all x1, blocking collectives, per_device(): lax.all_to_all(blocks, 'pa', split_axis=0, concat_axis=0, tiled=True)  55.7 us
    pallas_call x1, Pallas kernels, covariances(): pl.pallas_call(functools.partial(covariance_kernel, total_gates), out_sha...  5.22 us
    pallas_call x1, Pallas kernels, doppler(): pl.pallas_call(doppler_kernel, out_shape=jax.ShapeDtypeStruct((2 * pulses...  2.68 us

profile of v8, /device:TPU:0, one launch (start us, length us, event | category | flops | bytes accessed | tf_op | source)
XLA Modules:
  0.0 126.1 jit_solution(6314484961077527694)
XLA Ops:
  0.0 2.2 %repack.1 = (bf16[16,2,32,16,128]{4,3,2,1,0:T(8,128)(2,1)S(1)}, bf16[384,256]{1,0:T(8,128)(2,1)S(1)}) custom-call(f32[1,256]{1,0:T(1,128)} %bitcast.7, bf16[2,16,32,16,128]{4,3,2,1,0:T(8,128)(2,1)} %bitcast.6), custom_call_target="tpu_custom_call" | custom-call | tf_op jit(solution)/shard_map/repack/pallas_call | solution.py:125
  2.2 0.0 copy-start
  2.3 55.7 %all_to_all.10.samples_ref = bf16[16,2,32,16,128]{4,3,2,1,0:T(8,128)(2,1)S(1)} all-to-all(bf16[16,2,32,16,128]{4,3,2,1,0:T(8,128)(2,1)S(1)} %get-tuple-element.8), channel_id=1, replica_groups=mesh['pa'=16,'row'=8] {'pa'}, dimensions={0} | all-to-all | bytes 8388608 | tf_op jit(solution)/shard_map/all_to_all | solution.py:201
  58.0 0.0 copy-done
  58.0 2.7 %doppler.1 = bf16[512,32,128]{2,1,0:T(8,128)(2,1)S(1)} custom-call(bf16[256,256]{1,0:T(8,128)(2,1)S(1)} %copy-done, bf16[16,2,32,16,128]{4,3,2,1,0:T(8,128)(2,1)S(1)} %all_to_all.10.samples_ref), custom_call_target="tpu_custom_call" | custom-call | tf_op jit(solution)/shard_map/doppler/pallas_call | solution.py:69
  60.6 60.2 %all_to_all.11 = bf16[128,2,2,32,128]{4,3,2,1,0:T(8,128)(2,1)S(1)} all-to-all(bf16[128,2,2,32,128]{4,3,2,1,0:T(8,128)(2,1)S(1)} %bitcast.5), channel_id=1, replica_groups=mesh['pa'=16,'row'=8] {'pa','row'}, dimensions={0} | all-to-all | bytes 8388608 | tf_op jit(solution)/shard_map/all_to_all | solution.py:204
  120.9 5.2 %covariances.1 = f32[2,2,128,128]{3,2,1,0:T(8,128)} custom-call(bf16[384,256]{1,0:T(8,128)(2,1)S(1)} %get-tuple-element.7.bands_ref, bf16[16,8,2,2,32,128]{5,4,3,2,1,0:T(8,128)(2,1)S(1)} %bitcast.4), custom_call_target="tpu_custom_call" | custom-call | tf_op jit(solution)/shard_map/covariances/pallas_call | solution.py:180
Async XLA Ops:
  2.2 55.7 %copy-start = (bf16[256,256]{1,0:T(8,128)(2,1)S(1)}, bf16[256,256]{1,0:T(8,128)(2,1)}, u32[]{:S(2)}) copy-start(bf16[256,256]{1,0:T(8,128)(2,1)} %constant.2.clone.rows_ref) | copy-start | bytes 393220

commit v9 on v8

--- a/solution.py
+++ b/solution.py
@@ -140,7 +140,7 @@
     )(phase, echoes)
 
 
-def covariance_kernel(total_gates, bands_ref, samples_ref, out_ref):
+def covariance_kernel(total_gates, bands_ref, samples_ref, out_ref, result, sems):
     pa_count, row_count, bins, _, gates, n = samples_ref.shape
     bands = bands_ref[...]
     tile = bands.shape[1] // 2
@@ -171,8 +171,11 @@
         gram = lax.dot_general(
             one, one, (((0,), (0,)), ((), ())), preferred_element_type=jnp.float32
         )
-        out_ref[b, 0] = (gram[:n, :n] + gram[n:, n:]) / total_gates
-        out_ref[b, 1] = (gram[n:, :n] - gram[:n, n:]) / total_gates
+        result[b, 0] = (gram[:n, :n] + gram[n:, n:]) / total_gates
+        result[b, 1] = (gram[n:, :n] - gram[:n, n:]) / total_gates
+        pltpu.make_async_copy(result.at[b], out_ref.at[b], sems.at[b]).start()
+    for b in range(bins):
+        pltpu.make_async_copy(result.at[b], out_ref.at[b], sems.at[b]).wait()
 
 
 def covariances(bands, samples, total_gates):
@@ -181,7 +184,11 @@
         functools.partial(covariance_kernel, total_gates),
         out_shape=jax.ShapeDtypeStruct((bins, 2, element_count, element_count), jnp.float32),
         in_specs=[pl.BlockSpec(memory_space=pltpu.VMEM)] * 2,
-        out_specs=pl.BlockSpec(memory_space=pltpu.VMEM),
+        out_specs=pl.BlockSpec(memory_space=pltpu.HBM),
+        scratch_shapes=[
+            pltpu.VMEM((bins, 2, element_count, element_count), jnp.float32),
+            pltpu.SemaphoreType.DMA((bins,)),
+        ],
         compiler_params=pltpu.CompilerParams(vmem_limit_bytes=24 << 20),
         name="covariances",
     )(bands, samples)

time: 126 us -> 126 us (level)
  no operation moved by 1% of the time
where the time goes in v9:
time: 126 us
  blocking collectives  116 us (92%)
  Pallas kernels  10.2 us (8%)
    all_to_all x1, blocking collectives, per_device(): lax.all_to_all(spectrum, ('pa', 'row'), split_axis=0, concat_axis=0, tile...  60.2 us
    all_to_all x1, blocking collectives, per_device(): lax.all_to_all(blocks, 'pa', split_axis=0, concat_axis=0, tiled=True)  55.7 us
    pallas_call x1, Pallas kernels, covariances(): pl.pallas_call(functools.partial(covariance_kernel, total_gates), out_sha...  5.23 us
    pallas_call x1, Pallas kernels, doppler(): pl.pallas_call(doppler_kernel, out_shape=jax.ShapeDtypeStruct((2 * pulses...  2.68 us

profile of v9, /device:TPU:0, one launch (start us, length us, event | category | flops | bytes accessed | tf_op | source)
XLA Modules:
  0.0 126.1 jit_solution(3654893548563733184)
XLA Ops:
  0.0 2.2 %repack.1 = (bf16[16,2,32,16,128]{4,3,2,1,0:T(8,128)(2,1)S(1)}, bf16[384,256]{1,0:T(8,128)(2,1)S(1)}) custom-call(f32[1,256]{1,0:T(1,128)} %bitcast.7, bf16[2,16,32,16,128]{4,3,2,1,0:T(8,128)(2,1)} %bitcast.6), custom_call_target="tpu_custom_call" | custom-call | tf_op jit(solution)/shard_map/repack/pallas_call | solution.py:125
  2.2 0.0 copy-start
  2.3 55.7 %all_to_all.10.samples_ref = bf16[16,2,32,16,128]{4,3,2,1,0:T(8,128)(2,1)S(1)} all-to-all(bf16[16,2,32,16,128]{4,3,2,1,0:T(8,128)(2,1)S(1)} %get-tuple-element.8), channel_id=1, replica_groups=mesh['pa'=16,'row'=8] {'pa'}, dimensions={0} | all-to-all | bytes 8388608 | tf_op jit(solution)/shard_map/all_to_all | solution.py:208
  58.0 0.0 copy-done
  58.0 2.7 %doppler.1 = bf16[512,32,128]{2,1,0:T(8,128)(2,1)S(1)} custom-call(bf16[256,256]{1,0:T(8,128)(2,1)S(1)} %copy-done, bf16[16,2,32,16,128]{4,3,2,1,0:T(8,128)(2,1)S(1)} %all_to_all.10.samples_ref), custom_call_target="tpu_custom_call" | custom-call | tf_op jit(solution)/shard_map/doppler/pallas_call | solution.py:69
  60.6 60.2 %all_to_all.11 = bf16[128,2,2,32,128]{4,3,2,1,0:T(8,128)(2,1)S(1)} all-to-all(bf16[128,2,2,32,128]{4,3,2,1,0:T(8,128)(2,1)S(1)} %bitcast.5), channel_id=1, replica_groups=mesh['pa'=16,'row'=8] {'pa','row'}, dimensions={0} | all-to-all | bytes 8388608 | tf_op jit(solution)/shard_map/all_to_all | solution.py:211
  120.9 5.2 %covariances.1 = f32[2,2,128,128]{3,2,1,0:T(8,128)} custom-call(bf16[384,256]{1,0:T(8,128)(2,1)S(1)} %get-tuple-element.7.bands_ref, bf16[16,8,2,2,32,128]{5,4,3,2,1,0:T(8,128)(2,1)S(1)} %bitcast.4), custom_call_target="tpu_custom_call" | custom-call | tf_op jit(solution)/shard_map/covariances/pallas_call | solution.py:183
Async XLA Ops:
  2.2 55.7 %copy-start = (bf16[256,256]{1,0:T(8,128)(2,1)S(1)}, bf16[256,256]{1,0:T(8,128)(2,1)}, u32[]{:S(2)}) copy-start(bf16[256,256]{1,0:T(8,128)(2,1)} %constant.2.clone.rows_ref) | copy-start | bytes 393220

commit v10 on v8

--- a/solution.py
+++ b/solution.py
@@ -165,12 +165,15 @@
         sums = [x if y is None else x + y for x, y in zip(sums, carried + [None])]
         carried = sums[1:]
         filtered.append(sums[0].astype(jnp.bfloat16))
-    filtered = jnp.concatenate(filtered, axis=0)
+    middle = len(filtered) // 2
+    halves = [jnp.concatenate(h, axis=0) for h in (filtered[:middle], filtered[middle:])]
     for b in range(bins):
-        one = filtered[:, b * 2 * n : (b + 1) * 2 * n]
-        gram = lax.dot_general(
-            one, one, (((0,), (0,)), ((), ())), preferred_element_type=jnp.float32
-        )
+        ones = [half[:, b * 2 * n : (b + 1) * 2 * n] for half in halves]
+        grams = [
+            lax.dot_general(one, one, (((0,), (0,)), ((), ())), preferred_element_type=jnp.float32)
+            for one in ones
+        ]
+        gram = grams[0] + grams[1]
         out_ref[b, 0] = (gram[:n, :n] + gram[n:, n:]) / total_gates
         out_ref[b, 1] = (gram[n:, :n] - gram[:n, n:]) / total_gates
 

time: 126 us -> 126 us (level)
  no operation moved by 1% of the time
where the time goes in v10:
time: 126 us
  blocking collectives  116 us (92%)
  Pallas kernels  10.1 us (8%)
    all_to_all x1, blocking collectives, per_device(): lax.all_to_all(spectrum, ('pa', 'row'), split_axis=0, concat_axis=0, tile...  60.2 us
    all_to_all x1, blocking collectives, per_device(): lax.all_to_all(blocks, 'pa', split_axis=0, concat_axis=0, tiled=True)  55.7 us
    pallas_call x1, Pallas kernels, covariances(): pl.pallas_call(functools.partial(covariance_kernel, total_gates), out_sha...  5.22 us
    pallas_call x1, Pallas kernels, doppler(): pl.pallas_call(doppler_kernel, out_shape=jax.ShapeDtypeStruct((2 * pulses...  2.68 us

profile of v10, /device:TPU:0, one launch (start us, length us, event | category | flops | bytes accessed | tf_op | source)
XLA Modules:
  0.0 126.1 jit_solution(9434346954837531622)
XLA Ops:
  0.0 2.2 %repack.1 = (bf16[16,2,32,16,128]{4,3,2,1,0:T(8,128)(2,1)S(1)}, bf16[384,256]{1,0:T(8,128)(2,1)S(1)}) custom-call(f32[1,256]{1,0:T(1,128)} %bitcast.7, bf16[2,16,32,16,128]{4,3,2,1,0:T(8,128)(2,1)} %bitcast.6), custom_call_target="tpu_custom_call" | custom-call | tf_op jit(solution)/shard_map/repack/pallas_call | solution.py:125
  2.2 0.0 copy-start
  2.3 55.7 %all_to_all.10.samples_ref = bf16[16,2,32,16,128]{4,3,2,1,0:T(8,128)(2,1)S(1)} all-to-all(bf16[16,2,32,16,128]{4,3,2,1,0:T(8,128)(2,1)S(1)} %get-tuple-element.8), channel_id=1, replica_groups=mesh['pa'=16,'row'=8] {'pa'}, dimensions={0} | all-to-all | bytes 8388608 | tf_op jit(solution)/shard_map/all_to_all | solution.py:204
  58.0 0.0 copy-done
  58.0 2.7 %doppler.1 = bf16[512,32,128]{2,1,0:T(8,128)(2,1)S(1)} custom-call(bf16[256,256]{1,0:T(8,128)(2,1)S(1)} %copy-done, bf16[16,2,32,16,128]{4,3,2,1,0:T(8,128)(2,1)S(1)} %all_to_all.10.samples_ref), custom_call_target="tpu_custom_call" | custom-call | tf_op jit(solution)/shard_map/doppler/pallas_call | solution.py:69
  60.6 60.2 %all_to_all.11 = bf16[128,2,2,32,128]{4,3,2,1,0:T(8,128)(2,1)S(1)} all-to-all(bf16[128,2,2,32,128]{4,3,2,1,0:T(8,128)(2,1)S(1)} %bitcast.5), channel_id=1, replica_groups=mesh['pa'=16,'row'=8] {'pa','row'}, dimensions={0} | all-to-all | bytes 8388608 | tf_op jit(solution)/shard_map/all_to_all | solution.py:207
  120.9 5.2 %covariances.1 = f32[2,2,128,128]{3,2,1,0:T(8,128)} custom-call(bf16[384,256]{1,0:T(8,128)(2,1)S(1)} %get-tuple-element.7.bands_ref, bf16[16,8,2,2,32,128]{5,4,3,2,1,0:T(8,128)(2,1)S(1)} %bitcast.4), custom_call_target="tpu_custom_call" | custom-call | tf_op jit(solution)/shard_map/covariances/pallas_call | solution.py:183
Async XLA Ops:
  2.2 55.7 %copy-start = (bf16[256,256]{1,0:T(8,128)(2,1)S(1)}, bf16[256,256]{1,0:T(8,128)(2,1)}, u32[]{:S(2)}) copy-start(bf16[256,256]{1,0:T(8,128)(2,1)} %constant.2.clone.rows_ref) | copy-start | bytes 393220
